TPU v7x, 256 devices: a whole 4x4x8 slice. The times are simulated.
256 devices in a mesh: dp: 16 (over z_hi, y, core), slab: 16 (over z_lo, x).
Axes of the slice: x: 4, y: 4, z: 8 (z_hi: 2, z_lo: 4; z = z_hi * 4 + z_lo), core: 2. Of those that a mesh axis runs over, the one named last changes fastest.
Arguments:
- features: bfloat16 [16, 160, 64, 256], P('dp', 'slab'), may hold values from -6 to 6
- cotangent: bfloat16 [16, 160, 64, 256], P('dp', 'slab'), may hold values from -6 to 6
- neighbour_table: int32 [16, 160, 27], P('dp', 'slab'), may hold values from 0 to 14, as said below
- send_lists: int32 [16, 16, 2, 2], P('dp', 'slab'), may hold values from 0 to 10, as said below
- block_counts: int32 [16, 16], P('dp', 'slab'), may hold values from 5 to 10, as said below
- weight_one: bfloat16 [6912, 256], replicated, may hold values from -0.078125 to 0.078125
- weight_two: bfloat16 [6912, 256], replicated, may hold values from -0.078125 to 0.078125
Outputs:
- output: bfloat16 [16, 160, 64, 256], P('dp', 'slab')
- grad_features: bfloat16 [16, 160, 64, 256], P('dp', 'slab')
- grad_one: float32 [6912, 256], P('slab', 'dp')
- grad_two: float32 [6912, 256], P('slab', 'dp')
Inputs may be any that keep to these rules, and one draw needn't show every extreme that they name: `neighbour_table`: row b of slab l = b // 10 lists where the block at each of the 27 block offsets lies, in the numbering of the gathered step; rows of padding slots hold only 14. The relation is symmetric: a block that names another at an offset is named by it at the opposite offset. `send_lists`: list 0 of a slab names, in increasing order, its occupied blocks in its first block-plane, the ones the previous slab can touch; list 1 those of its last block-plane; 10 fills the remaining slots. `block_counts`: slots at and above a slab's count are padding.
All inputs are finite; a program needn't handle non-finite values.
Results may differ from a plain program's by a relative error of at most 0.013.
Values may be sent and summed in bfloat16 or wider, within the bound.
A program may use at most 128 MiB of HBM per device.

v0:
```python
import math

import jax
import jax.numpy as jnp
from jax import lax
from jax.experimental import pallas as pl
from jax.experimental.pallas import tpu as pltpu
from jax.sharding import PartitionSpec as P

F32 = jnp.float32
BF16 = jnp.bfloat16
MESH = pl.DeviceIdType.MESH
ROWS = 160
C = 256
NT = (((1,), (1,)), ((), ()))
TN = (((0,), (0,)), ((), ()))


def dot(a, b, dims=(((1,), (0,)), ((), ()))):
    return lax.dot_general(a, b, dims, preferred_element_type=F32)


def kernel(
    factor,
    counts, lists, table_ref, feat_ref, cot_ref, w1_hbm, w2_hbm,
    out_ref, gf_ref, g1_ref, g2_ref,
    w1, w2, nat, t_own, t_ext, pack, hrecv, t_own2, pack2, hrecv2, sel, win, acc_a, acc_b,
    hid_t, psend, precv, xy, recv_a, recv_b, sum_a, sum_b, recv_a2, recv_b2, zsend, zrecv, fin_t, fin_recv,
    wsem, hs, hr, ps, pr, as_, ar, bs, br, a2s, a2r, b2s, b2r, zs, zr, fs, fr,
):
    dp = lax.axis_index("dp")
    slab = lax.axis_index("slab")
    core = dp % 2
    y = dp // 2 % 4
    z_hi = dp // 8
    x = slab % 4
    z_lo = slab // 4
    z = z_hi * 4 + z_lo

    def dev(x_=x, y_=y, z_=z, core_=core):
        return ((z_ // 4) * 8 + y_ * 2 + core_, (z_ % 4) * 4 + x_)

    after = (slab + 1) % 16
    before = (slab + 15) % 16
    peer = dev(core_=1 - core)
    x_peers = [dev(x_=(x + d) % 4) for d in range(1, 4)]
    y_peers = [dev(y_=(y + d) % 4) for d in range(1, 4)]
    z_peers = [dev(z_=(z + d) % 8) for d in range(1, 8)]
    yc = y * 2 + core
    f_peers = [dev(y_=(yc + d) % 8 // 2, core_=(yc + d) % 2) for d in range(1, 8)]

    barrier = pltpu.get_barrier_semaphore()
    everyone = [(dp, after), (dp, before), peer] + x_peers + y_peers + z_peers + f_peers
    for d in everyone:
        pl.semaphore_signal(barrier, inc=1, device_id=d, device_id_type=MESH)

    load_w1 = pltpu.make_async_copy(w1_hbm, w1, wsem.at[0])
    load_w2 = pltpu.make_async_copy(w2_hbm, w2, wsem.at[1])
    load_w1.start()
    load_w2.start()

    def remote(src, dst, send, recv, to):
        return pltpu.make_async_remote_copy(
            src_ref=src, dst_ref=dst, send_sem=send, recv_sem=recv, device_id=to, device_id_type=MESH
        )

    row = lax.broadcasted_iota(jnp.int32, (640, 1), 0)
    present = jnp.where(row < counts[0, 0] * 64, 1.0, 0.0)
    for part, value in (
        (0, feat_ref[...].reshape(640, C).astype(F32) * present),
        (2, cot_ref[...].reshape(640, C).astype(F32)),
    ):
        nat[part], nat[part + 1] = value[:, 0:128], value[:, 128:]
    for k in range(4):
        part = jnp.concatenate([nat[n, pl.ds(k, ROWS, stride=4), :] for n in range(4)], axis=1)
        part = part.astype(BF16).reshape(10, 16, 2 * C)
        t_own[:, k] = part
        t_ext[0:10, k] = part

    def pack_edges(source, target):
        for side in range(2):
            inside = jnp.where(side == 0, slab > 0, slab < 15)
            for q in range(2):
                named = lists[side, q]
                keep = jnp.where(inside & (named < 10), 1.0, 0.0).astype(BF16)
                target[side, q] = source[jnp.minimum(named, 9)] * keep

    def halo(source, target, e):
        return (
            remote(source.at[1], target.at[0], hs.at[e, 0], hr.at[e, 0], (dp, after)),
            remote(source.at[0], target.at[1], hs.at[e, 1], hr.at[e, 1], (dp, before)),
        )

    pack_edges(t_own, pack)
    pl.semaphore_wait(barrier, len(everyone))
    first = halo(pack, hrecv, 0)
    for copy in first:
        copy.start()

    r = lax.broadcasted_iota(jnp.int32, (ROWS, 1), 0)
    spread = (r // 16 == lax.broadcasted_iota(jnp.int32, (ROWS, 10), 1)).astype(F32)
    rows_of = dot(spread, table_ref[...].astype(F32))
    i_of, j_of = r // 4 % 4, r % 4
    lane = lax.broadcasted_iota(jnp.int32, (ROWS, 224), 1)

    def options(position, step):
        if step == 0:
            return [(0, position == 0), (1, position > 0)]
        if step == 1:
            return [(1, None)]
        return [(1, position < 3), (2, position == 3)]

    for dx in range(3):
        for dy in range(3):
            spot = (i_of + dx + 3) % 4 * 4 + (j_of + dy + 3) % 4
            for bz in range(3):
                block = None
                for bx, cond_x in options(i_of, dx):
                    for by, cond_y in options(j_of, dy):
                        n = 9 * bx + 3 * by + bz
                        value = rows_of[:, n : n + 1]
                        cond = cond_x if cond_y is None else cond_y if cond_x is None else cond_x & cond_y
                        block = value if block is None else jnp.where(cond, value, block)
                source = block.astype(jnp.int32) * 16 + spot
                sel[dx * 3 + dy, bz] = jnp.where(lane == source, 1.0, 0.0).astype(BF16)

    def finish_halo(copies, received, ext):
        for copy in copies:
            copy.wait_recv()
        ext[10:14] = received[...].reshape(4, 4, 16, 2 * C)

    def build(ext):
        def one(g, carry):
            for spot in range(6):
                k = (spot + 3) % 4
                bz = 0 if spot == 0 else 2 if spot == 5 else 1
                win[g, spot] = dot(sel[g, bz], ext[:, k].reshape(224, 2 * C)).astype(BF16)
            return carry

        lax.fori_loop(0, 9, one, 0)

    def view(g, dz, low):
        return win[g, dz : dz + 4, :, low : low + C].reshape(640, C)

    def convolve(w_fwd, w_bwd):
        acc_a[...] = jnp.zeros_like(acc_a)
        acc_b[...] = jnp.zeros_like(acc_b)

        def one(g, carry):
            left = jnp.concatenate([view(g, dz, 0) for dz in range(3)], axis=1)
            acc_a[...] += dot(left, w_fwd[g].reshape(3 * C, C))
            left = jnp.concatenate([view(g, dz, C) for dz in range(3)], axis=1)
            right = jnp.concatenate([w_bwd[8 - g, 2 - dz] for dz in range(3)], axis=1)
            acc_b[...] += dot(left, right, NT)
            return carry

        lax.fori_loop(0, 9, one, 0)

    load_w1.wait()
    load_w2.wait()
    finish_halo(first, hrecv, t_ext)
    build(t_ext)
    convolve(w1, w2)

    hidden = jnp.maximum(acc_a[...], 0.0)
    rounded = hidden.astype(BF16)
    grad_hidden = jnp.where(rounded > 0, acc_b[...].astype(BF16), jnp.zeros((), BF16))
    hid_t[...] = hidden.T.astype(BF16)
    for k in range(4):
        rows = slice(k * ROWS, (k + 1) * ROWS)
        t_own2[:, k, :, 0:C] = rounded[rows].reshape(10, 16, C)
        t_own2[:, k, :, C:] = grad_hidden[rows].reshape(10, 16, C)
        t_ext[0:10, k, :, 0:C] = rounded[rows].reshape(10, 16, C)
        t_ext[0:10, k, :, C:] = grad_hidden[rows].reshape(10, 16, C)
    pack_edges(t_own2, pack2)
    second = halo(pack2, hrecv2, 1)
    for copy in second:
        copy.start()

    def to_peer(g):
        part = pl.ds(pl.multiple_of(g * 768, 768), 768)
        return remote(psend.at[part], precv.at[part], ps.at[g], pr.at[g], peer)

    gh_rows = jnp.concatenate([t_own2[:, k, :, C:].reshape(ROWS, C) for k in range(4)], axis=0)

    def grads(g, carry):
        for dz in range(3):
            one = dot(view(g, dz, 0), gh_rows, TN)
            two = dot(hid_t[...], view(8 - g, 2 - dz, C))
            rows = pl.ds(pl.multiple_of(g * 768 + dz * 256, 256), 256)
            xy[rows] = jnp.where(core == 0, one, two).astype(BF16)
            psend[rows] = jnp.where(core == 0, two, one).astype(BF16)
        to_peer(g).start()
        return carry

    lax.fori_loop(0, 9, grads, 0)
    xy[6912:6928] = jnp.zeros((16, C), BF16)

    def join(g, carry):
        to_peer(g).wait_recv()
        for dz in range(3):
            rows = pl.ds(pl.multiple_of(g * 768 + dz * 256, 256), 256)
            xy[rows] = (xy[rows].astype(F32) + precv[rows].astype(F32)).astype(BF16)
        return carry

    lax.fori_loop(0, 9, join, 0)

    def rows_at(start, size):
        return pl.ds(pl.multiple_of(start, 16), size)

    def copy_a(d, zl):
        where = rows_at(432 * (zl * 4 + (x + d) % 4), 432)
        return remote(xy.at[where], recv_a.at[d - 1, zl], as_.at[d - 1, zl], ar.at[d - 1, zl], x_peers[d - 1])

    def copy_b(d, s):
        where = rows_at(432 * (8 + s) + 112 * ((y + d) % 4), 112)
        return remote(xy.at[where], recv_b.at[d - 1, s], bs.at[d - 1, s], br.at[d - 1, s], y_peers[d - 1])

    stage_a = [copy_a(d, zl) for d in (2, 1, 3) for zl in range(2)]
    stage_b = [copy_b(d, s) for d in (2, 1, 3) for s in range(8)]
    for copy in stage_a + stage_b:
        copy.start()

    finish_halo(second, hrecv2, t_ext)
    build(t_ext)
    convolve(w2, w1)
    for k in range(4):
        rows = slice(k * ROWS, (k + 1) * ROWS)
        for n, acc in enumerate((acc_a, acc_b)):
            for half in range(2):
                nat[2 * n + half, pl.ds(k, ROWS, stride=4), :] = acc[rows, half * 128 : half * 128 + 128]
    masked = feat_ref[...].reshape(640, C).astype(F32) * present
    out_ref[...] = (jnp.concatenate([nat[0], nat[1]], axis=1) + masked).astype(BF16).reshape(10, 64, C)
    upstream = cot_ref[...].reshape(640, C).astype(F32)
    gf_ref[...] = ((upstream + jnp.concatenate([nat[2], nat[3]], axis=1)) * present).astype(BF16).reshape(10, 64, C)

    def total(parts):
        value = parts[0].astype(F32)
        for part in parts[1:]:
            value = value + part.astype(F32)
        return value

    for copy in stage_a:
        copy.wait_recv()

    def add_a(n, carry):
        zl, third = n // 3, n % 3
        inner = rows_at(third * 144, 144)
        own = xy[rows_at(432 * (zl * 4 + x) + third * 144, 144)]
        sum_a[zl, inner] = total([own] + [recv_a[d, zl, inner] for d in range(3)]).astype(BF16)
        return carry

    lax.fori_loop(0, 6, add_a, 0)
    for zl in range(2):
        sum_a[zl, 432:448] = jnp.zeros((16, C), BF16)
    stage_a2 = [
        remote(
            sum_a.at[:, rows_at(112 * ((y + d) % 4), 112)], recv_a2.at[d - 1], a2s.at[d - 1], a2r.at[d - 1], y_peers[d - 1]
        )
        for d in (2, 1, 3)
    ]
    for copy in stage_a2:
        copy.start()

    for copy in stage_b:
        copy.wait_recv()

    def add_b(s, carry):
        own = xy[rows_at(432 * (8 + s) + 112 * y, 112)]
        sum_b[s // 4, s % 4] = total([own] + [recv_b[d, s] for d in range(3)]).astype(BF16)
        return carry

    lax.fori_loop(0, 8, add_b, 0)
    stage_b2 = [
        remote(sum_b.at[:, (x + d) % 4], recv_b2.at[d - 1], b2s.at[d - 1], b2r.at[d - 1], x_peers[d - 1])
        for d in (2, 1, 3)
    ]
    for copy in stage_b2:
        copy.start()

    for copy in stage_a2:
        copy.wait_recv()
    for zl in range(2):
        own = sum_a[zl, rows_at(112 * y, 112)]
        full = total([own] + [recv_a2[d, zl] for d in range(3)]).astype(BF16)
        zsend[0, zl], zsend[1, zl] = full[:, 0:128], full[:, 128:]
    for copy in stage_b2:
        copy.wait_recv()
    for zl in range(2):
        own = sum_b[zl, x]
        full = total([own] + [recv_b2[d, zl] for d in range(3)]).astype(BF16)
        zsend[0, 2 + zl], zsend[1, 2 + zl] = full[:, 0:128], full[:, 128:]

    stage_z = []
    for d in (4, 3, 5, 2, 6, 1, 7):
        to = (z + d) % 8
        stage_z.append(remote(zsend.at[to // 4, to % 4], zrecv.at[d - 1], zs.at[d - 1], zr.at[d - 1], z_peers[d - 1]))
    for copy in stage_z:
        copy.start()
    for copy in stage_z:
        copy.wait_recv()
    whole = total([zsend[z_hi, z_lo]] + [zrecv[d] for d in range(7)]) * factor
    padded = jnp.concatenate([whole, jnp.zeros((16, 128), F32)], axis=0)
    fin_t[...] = padded.T.reshape(8, 16, 128)

    stage_f = []
    for d in range(1, 8):
        to = (yc + d) % 8
        stage_f.append(remote(fin_t.at[to], fin_recv.at[d - 1], fs.at[d - 1], fr.at[d - 1], f_peers[d - 1]))
    for copy in stage_f:
        copy.start()
    for copy in stage_f:
        copy.wait_recv()

    def place(value, source):
        part = value.T[0:112]
        for src_core, target in ((0, g1_ref), (1, g2_ref)):
            for src_y in range(4):
                size = 112 if src_y < 3 else 96

                @pl.when(source == src_y * 2 + src_core)
                def _():
                    target[112 * src_y : 112 * src_y + size] = part[0:size]

    place(fin_t[yc], yc)
    for d in range(1, 8):
        place(fin_recv[d - 1], (yc + 8 - d) % 8)

    for copy in list(first) + list(second) + stage_a + stage_b + stage_a2 + stage_b2 + stage_z + stage_f:
        copy.wait_send()

    def drain(g, carry):
        to_peer(g).wait_send()
        return carry

    lax.fori_loop(0, 9, drain, 0)


def per_device(features, cotangent, neighbour_table, send_lists, block_counts, weight_one, weight_two):
    factor = 1.0 / math.sqrt(lax.axis_size("dp") * lax.axis_size("slab") * 10 * 64)
    smem = pl.BlockSpec(memory_space=pltpu.SMEM)
    vmem = pl.BlockSpec(memory_space=pltpu.VMEM)
    hbm = pl.BlockSpec(memory_space=pl.ANY)
    dma = pltpu.SemaphoreType.DMA
    outs = pl.pallas_call(
        lambda *refs: kernel(factor, *refs),
        out_shape=(
            jax.ShapeDtypeStruct((10, 64, C), BF16),
            jax.ShapeDtypeStruct((10, 64, C), BF16),
            jax.ShapeDtypeStruct((432, 16), F32),
            jax.ShapeDtypeStruct((432, 16), F32),
        ),
        in_specs=[smem, smem, vmem, vmem, vmem, hbm, hbm],
        out_specs=(vmem, vmem, vmem, vmem),
        scratch_shapes=[
            pltpu.VMEM((9, 3, C, C), BF16),
            pltpu.VMEM((9, 3, C, C), BF16),
            pltpu.VMEM((4, 640, 128), F32),
            pltpu.VMEM((10, 4, 16, 2 * C), BF16),
            pltpu.VMEM((14, 4, 16, 2 * C), BF16),
            pltpu.VMEM((2, 2, 4, 16, 2 * C), BF16),
            pltpu.VMEM((2, 2, 4, 16, 2 * C), BF16),
            pltpu.VMEM((10, 4, 16, 2 * C), BF16),
            pltpu.VMEM((2, 2, 4, 16, 2 * C), BF16),
            pltpu.VMEM((2, 2, 4, 16, 2 * C), BF16),
            pltpu.VMEM((9, 3, ROWS, 224), BF16),
            pltpu.VMEM((9, 6, ROWS, 2 * C), BF16),
            pltpu.VMEM((640, C), F32),
            pltpu.VMEM((640, C), F32),
            pltpu.VMEM((C, 640), BF16),
            pltpu.VMEM((6912, C), BF16),
            pltpu.VMEM((6912, C), BF16),
            pltpu.VMEM((6928, C), BF16),
            pltpu.VMEM((3, 2, 432, C), BF16),
            pltpu.VMEM((3, 8, 112, C), BF16),
            pltpu.VMEM((2, 448, C), BF16),
            pltpu.VMEM((2, 4, 112, C), BF16),
            pltpu.VMEM((3, 2, 112, C), BF16),
            pltpu.VMEM((3, 2, 112, C), BF16),
            pltpu.VMEM((2, 4, 112, 128), BF16),
            pltpu.VMEM((7, 112, 128), BF16),
            pltpu.VMEM((8, 16, 128), F32),
            pltpu.VMEM((7, 16, 128), F32),
            dma((2,)),
            dma((2, 2)),
            dma((2, 2)),
            dma((9,)),
            dma((9,)),
            dma((3, 2)),
            dma((3, 2)),
            dma((3, 8)),
            dma((3, 8)),
            dma((3,)),
            dma((3,)),
            dma((3,)),
            dma((3,)),
            dma((7,)),
            dma((7,)),
            dma((7,)),
            dma((7,)),
        ],
        compiler_params=pltpu.CompilerParams(
            collective_id=0, has_side_effects=True, vmem_limit_bytes=60 * 1024 * 1024
        ),
        name="step",
    )(
        block_counts,
        send_lists[0, 0],
        neighbour_table[0],
        features[0],
        cotangent[0],
        weight_one.reshape(9, 3, C, C),
        weight_two.reshape(9, 3, C, C),
    )
    return (outs[0][None], outs[1][None], outs[2], outs[3])


def solution(mesh):
    in_specs = (
        P("dp", "slab", None, None),
        P("dp", "slab", None, None),
        P("dp", "slab", None),
        P("dp", "slab", None, None),
        P("dp", "slab"),
        P(),
        P(),
    )
    out_specs = (
        P("dp", "slab", None, None),
        P("dp", "slab", None, None),
        P("slab", "dp"),
        P("slab", "dp"),
    )
    return jax.shard_map(
        per_device, mesh=mesh, in_specs=in_specs, out_specs=out_specs, check_vma=False
    )
```

profile of v0, /device:TPU:1, one launch (start us, length us, event | category | flops | bytes accessed | tf_op | source)
XLA Modules:
  0.0 89.5 jit_solution(4434738545707161102)
XLA Ops:
  1.3 1.3 %copy.15 = s32[1,10,27]{2,1,0:T(8,128)} copy(s32[1,10,27]{2,0,1:T(1,128)} %param.9) | data formatting | bytes 2160
  2.6 80.2 %step.1 = (bf16[10,64,256]{2,1,0:T(8,128)(2,1)}, bf16[10,64,256]{2,1,0:T(8,128)(2,1)}, f32[432,16]{1,0:T(8,128)}, f32[432,16]{1,0:T(8,128)}) custom-call(s32[1,1]{1,0:T(1,128)S(6)} %copy.18.refs_0_, s32[2,2]{1,0:T(2,128)} %bitcast.17, s32[10,27]{1,0:T(8,128)} %bitcast.16, bf16[10,64,256]{2,1,0:T(8,128)(2,1)} %bitcast.12, bf16[10,64,256]{2,1,0:T(8,128)(2,1)} %bitcast.13, ...), custom_call_target="tpu_custom_call" | custom-call | tf_op jit(solution)/shard_map/step/pallas_call | solution.py:345
  82.7 1.7 %copy.11 = f32[432,16]{0,1:T(8,128)} copy(f32[432,16]{1,0:T(8,128)} %get-tuple-element.14) | data formatting | bytes 55296
  84.4 1.7 %copy.12 = f32[432,16]{0,1:T(8,128)} copy(f32[432,16]{1,0:T(8,128)} %get-tuple-element.15) | data formatting | bytes 55296
  86.1 1.7 %copy.19 = bf16[1,10,64,256]{3,2,1,0:T(8,128)(2,1)} copy(bf16[1,10,64,256]{3,2,1,0:T(8,128)(2,1)} %bitcast.15) | data formatting | bytes 655360
  87.8 1.7 %copy.20 = bf16[1,10,64,256]{3,2,1,0:T(8,128)(2,1)} copy(bf16[1,10,64,256]{3,2,1,0:T(8,128)(2,1)} %bitcast.14) | data formatting | bytes 655360
where the time goes:
time: 89.8 us; the launch traced here: 89.5 us
  Pallas kernels  80.2 us (89%)
  local copies, waits for them, and re-layouts  8.03 us (9%)
  between operations  1.29 us (1%)
    pallas_call x1, Pallas kernels, per_device(): pl.pallas_call(lambda *refs: kernel(factor, *refs), out_shape=(jax.ShapeD...  80.2 us
    unnamed x5, local copies, waits for them, and re-layouts  8.03 us

commit v1 on v0

v1 whole, which is shorter than its diff:
```python
import math

import jax
import jax.numpy as jnp
from jax import lax
from jax.experimental import pallas as pl
from jax.experimental.pallas import tpu as pltpu
from jax.sharding import PartitionSpec as P

F32 = jnp.float32
BF16 = jnp.bfloat16
MESH = pl.DeviceIdType.MESH
ROWS = 160
REACH = 176
C = 256
NT = (((1,), (1,)), ((), ()))
TN = (((0,), (0,)), ((), ()))


def dot(a, b, dims=(((1,), (0,)), ((), ()))):
    return lax.dot_general(a, b, dims, preferred_element_type=F32)


def kernel(
    factor,
    counts, lists, table_ref, feat_hbm, cot_hbm, w1_hbm, w2_hbm,
    out_hbm, gf_hbm, fin_ref,
    w1, w2, feat, cot, out_v, gf_v, nat, t_own, t_ext, pack, hrecv, t_own2, pack2, hrecv2, sel, win, acc_a, acc_b,
    hid_t, psend, precv, xy, relay_a, direct_a, summed_a, stage_a, relay_b, direct_b, summed_b, stage_b,
    sum_a, sum_b, recv_a2, recv_b2, zsend, zrecv, fin_t, fin_recv,
    lsem, osem, hs, hr, ps, pr, as_, ar, bs, br, a2s, a2r, b2s, b2r, zs, zr, fs, fr,
):
    dp = lax.axis_index("dp")
    slab = lax.axis_index("slab")
    core = dp % 2
    y = dp // 2 % 4
    z_hi = dp // 8
    x = slab % 4
    z_lo = slab // 4
    z = z_hi * 4 + z_lo

    def dev(x_=x, y_=y, z_=z, core_=core):
        return ((z_ // 4) * 8 + y_ * 2 + core_, (z_ % 4) * 4 + x_)

    after = (slab + 1) % 16
    before = (slab + 15) % 16
    peer = dev(core_=1 - core)
    x_peers = [dev(x_=(x + d) % 4) for d in range(1, 4)]
    y_peers = [dev(y_=(y + d) % 4) for d in range(1, 4)]
    z_peers = [dev(z_=(z + d) % 8) for d in range(1, 8)]
    yc = y * 2 + core
    f_peers = [dev(y_=(yc + d) % 8 // 2, core_=(yc + d) % 2) for d in range(1, 8)]

    barrier = pltpu.get_barrier_semaphore()
    everyone = [(dp, after), (dp, before), peer] + x_peers + y_peers + z_peers + f_peers
    for d in everyone:
        pl.semaphore_signal(barrier, inc=1, device_id=d, device_id_type=MESH)

    loads = [
        pltpu.make_async_copy(source, target, lsem.at[n])
        for n, (source, target) in enumerate(((feat_hbm, feat), (cot_hbm, cot), (w1_hbm, w1), (w2_hbm, w2)))
    ]
    for load in loads:
        load.start()

    def remote(src, dst, send, recv, to):
        return pltpu.make_async_remote_copy(
            src_ref=src, dst_ref=dst, send_sem=send, recv_sem=recv, device_id=to, device_id_type=MESH
        )

    row = lax.broadcasted_iota(jnp.int32, (640, 1), 0)
    present = jnp.where(row < counts[0, 0] * 64, 1.0, 0.0)
    loads[0].wait()
    loads[1].wait()
    for part, value in (
        (0, feat[...].reshape(640, C).astype(F32) * present),
        (2, cot[...].reshape(640, C).astype(F32)),
    ):
        nat[part], nat[part + 1] = value[:, 0:128], value[:, 128:]
    for k in range(4):
        part = jnp.concatenate([nat[n, pl.ds(k, ROWS, stride=4), :] for n in range(4)], axis=1)
        part = part.astype(BF16).reshape(10, 16, 2 * C)
        t_own[:, k] = part
        t_ext[0:10, k] = part

    def pack_edges(source, target):
        for side in range(2):
            inside = jnp.where(side == 0, slab > 0, slab < 15)
            for q in range(2):
                named = lists[side, q]
                keep = jnp.where(inside & (named < 10), 1.0, 0.0)
                block = source[jnp.minimum(named, 9)].astype(F32) * keep
                plane = [block[k, 12 * side : 12 * side + 4] for k in range(4)]
                target[side, q] = jnp.concatenate(plane, axis=0).astype(BF16)

    def halo(source, target, e):
        return (
            remote(source.at[1], target.at[0], hs.at[e, 0], hr.at[e, 0], (dp, after)),
            remote(source.at[0], target.at[1], hs.at[e, 1], hr.at[e, 1], (dp, before)),
        )

    pack_edges(t_own, pack)
    pl.semaphore_wait(barrier, len(everyone))
    first = halo(pack, hrecv, 0)
    for copy in first:
        copy.start()

    r = lax.broadcasted_iota(jnp.int32, (ROWS, 1), 0)
    spread = (r // 16 == lax.broadcasted_iota(jnp.int32, (ROWS, 10), 1)).astype(F32)
    rows_of = dot(spread, table_ref[...].reshape(10, 27).astype(F32))
    i_of, j_of = r // 4 % 4, r % 4
    lane = lax.broadcasted_iota(jnp.int32, (ROWS, REACH), 1)

    def options(position, step):
        if step == 0:
            return [(0, position == 0), (1, position > 0)]
        if step == 1:
            return [(1, None)]
        return [(1, position < 3), (2, position == 3)]

    for dx in range(3):
        for dy in range(3):
            spot_j = (j_of + dy + 3) % 4
            spot = (i_of + dx + 3) % 4 * 4 + spot_j
            for bz in range(3):
                block = None
                for bx, cond_x in options(i_of, dx):
                    for by, cond_y in options(j_of, dy):
                        n = 9 * bx + 3 * by + bz
                        value = rows_of[:, n : n + 1]
                        cond = cond_x if cond_y is None else cond_y if cond_x is None else cond_x & cond_y
                        block = value if block is None else jnp.where(cond, value, block)
                block = block.astype(jnp.int32)
                source = jnp.where(block < 10, block * 16 + spot, 160 + (block - 10) * 4 + spot_j)
                sel[dx * 3 + dy, bz] = jnp.where(lane == source, 1.0, 0.0).astype(BF16)

    def finish_halo(copies, received, ext):
        for copy in copies:
            copy.wait_recv()
        planes = [received[side, q].astype(F32) for side in range(2) for q in range(2)]
        for k in range(4):
            ext[10, k] = jnp.concatenate([plane[4 * k : 4 * k + 4] for plane in planes], axis=0).astype(BF16)

    def build(ext):
        def one(g, carry):
            for spot in range(6):
                k = (spot + 3) % 4
                bz = 0 if spot == 0 else 2 if spot == 5 else 1
                win[g, spot] = dot(sel[g, bz], ext[:, k].reshape(REACH, 2 * C)).astype(BF16)
            return carry

        lax.fori_loop(0, 9, one, 0)

    def view(g, dz, low):
        return win[g, pl.ds(dz, 4), :, low : low + C].reshape(640, C)

    def convolve(w_fwd, w_bwd, start, end):
        if start == 0:
            acc_a[...] = jnp.zeros_like(acc_a)
            acc_b[...] = jnp.zeros_like(acc_b)

        def one(g, carry):
            left = jnp.concatenate([view(g, dz, 0) for dz in range(3)], axis=1)
            acc_a[...] += dot(left, w_fwd[g].reshape(3 * C, C))
            left = jnp.concatenate([view(g, dz, C) for dz in range(3)], axis=1)
            right = jnp.concatenate([w_bwd[8 - g, 2 - dz] for dz in range(3)], axis=1)
            acc_b[...] += dot(left, right, NT)
            return carry

        lax.fori_loop(start, end, one, 0)

    finish_halo(first, hrecv, t_ext)
    build(t_ext)
    loads[2].wait()
    loads[3].wait()
    convolve(w1, w2, 0, 9)

    hidden = jnp.maximum(acc_a[...], 0.0)
    rounded = hidden.astype(BF16)
    grad_hidden = jnp.where(rounded > 0, acc_b[...].astype(BF16), jnp.zeros((), BF16))
    hid_t[...] = hidden.T.astype(BF16)
    for k in range(4):
        rows = slice(k * ROWS, (k + 1) * ROWS)
        t_own2[:, k, :, 0:C] = rounded[rows].reshape(10, 16, C)
        t_own2[:, k, :, C:] = grad_hidden[rows].reshape(10, 16, C)
        t_ext[0:10, k, :, 0:C] = rounded[rows].reshape(10, 16, C)
        t_ext[0:10, k, :, C:] = grad_hidden[rows].reshape(10, 16, C)
    pack_edges(t_own2, pack2)
    second = halo(pack2, hrecv2, 1)
    for copy in second:
        copy.start()

    def block_of(o):
        return pl.ds(pl.multiple_of(o * C, C), C)

    def to_peer(o):
        return remote(psend.at[block_of(o)], precv.at[block_of(o)], ps.at[o], pr.at[o], peer)

    gh_rows = jnp.concatenate([t_own2[:, k, :, C:].reshape(ROWS, C) for k in range(4)], axis=0)

    def grad_at(o):
        one = dot(view(o // 3, o % 3, 0), gh_rows, TN)
        two = dot(hid_t[...], view(8 - o // 3, 2 - o % 3, C))
        xy[block_of(o)] = jnp.where(core == 0, one, two).astype(BF16)
        psend[block_of(o)] = jnp.where(core == 0, two, one).astype(BF16)
        to_peer(o).start()

    def grads(n, carry):
        grad_at(n)
        grad_at(26 - n)
        return carry

    def join(o):
        to_peer(o).wait_recv()
        xy[block_of(o)] = (xy[block_of(o)].astype(F32) + precv[block_of(o)].astype(F32)).astype(BF16)

    def join_ends(n, carry):
        join(n)
        join(26 - n)
        return carry

    def join_middle(n, carry):
        join(n)
        return carry

    def rows_at(start, size):
        return pl.ds(pl.multiple_of(start, 16), size)

    def slab_rows(zl, owner_x):
        return rows_at(432 * (zl * 4 + owner_x), 432)

    def part_rows(zl, s, owner_y):
        return rows_at(432 * (zl * 4 + s) + 112 * owner_y, 112)

    LOW, HIGH = slice(0, 128), slice(128, 256)
    next_x, last_x, far_x = (x + 1) % 4, (x + 3) % 4, (x + 2) % 4
    next_y, last_y, far_y = (y + 1) % 4, (y + 3) % 4, (y + 2) % 4

    def first_copies(h):
        copies = {}
        for phase, (buf_a, buf_b) in enumerate(((relay_a, relay_b), (direct_a, direct_b))):
            for way in range(2):
                to_x, to_y = (x_peers[0], y_peers[0]) if way == 0 else (x_peers[2], y_peers[2])
                if phase == 0:
                    owner_x, owner_y, lanes = far_x, far_y, LOW if way == 0 else HIGH
                else:
                    owner_x, owner_y = (next_x, next_y) if way == 0 else (last_x, last_y)
                    lanes = HIGH if way == 0 else LOW
                copies[phase, way] = [
                    remote(
                        xy.at[slab_rows(h, owner_x), lanes], buf_a.at[h, way],
                        as_.at[h, phase, way], ar.at[h, phase, way], to_x,
                    )
                ] + [
                    remote(
                        xy.at[part_rows(3 - h, s, owner_y), lanes], buf_b.at[h, way, s],
                        bs.at[h, phase, way, s], br.at[h, phase, way, s], to_y,
                    )
                    for s in range(4)
                ]
        for way in range(2):
            to_x, to_y = (x_peers[0], y_peers[0]) if way == 0 else (x_peers[2], y_peers[2])
            copies[2, way] = [
                remote(stage_a.at[h, way], summed_a.at[h, way], as_.at[h, 2, way], ar.at[h, 2, way], to_x),
                remote(stage_b.at[h, way], summed_b.at[h, way], bs.at[h, 2, way, 0], br.at[h, 2, way, 0], to_y),
            ]
        return copies

    copies_of = [first_copies(0), first_copies(1)]

    def start_first(h):
        for phase in range(2):
            a0, b0 = copies_of[h][phase, 0], copies_of[h][phase, 1]
            for copy in [c for pair in zip(a0, b0) for c in pair]:
                copy.start()

    def total(*parts):
        value = parts[0].astype(F32)
        for part in parts[1:]:
            value = value + part.astype(F32)
        return value

    def pass_on(h):
        for way in range(2):
            for copy in copies_of[h][0, way]:
                copy.wait_recv()
        for way, lanes, owner_x, owner_y in ((0, LOW, next_x, next_y), (1, HIGH, last_x, last_y)):
            stage_a[h, way] = total(xy[slab_rows(h, owner_x), lanes], relay_a[h, way]).astype(BF16)
            for s in range(4):
                own = xy[part_rows(3 - h, s, owner_y), lanes]
                stage_b[h, way, s] = total(own, relay_b[h, way, s]).astype(BF16)
            for copy in copies_of[h][2, way]:
                copy.start()

    lax.fori_loop(0, 7, grads, 0)
    xy[6912:6928] = jnp.zeros((16, C), BF16)
    lax.fori_loop(7, 9, grads, 0)
    lax.fori_loop(0, 7, join_ends, 0)
    start_first(0)
    lax.fori_loop(9, 13, grads, 0)
    grad_at(13)
    lax.fori_loop(7, 20, join_middle, 0)
    start_first(1)

    finish_halo(second, hrecv2, t_ext)
    build(t_ext)
    pass_on(0)
    convolve(w2, w1, 0, 4)
    pass_on(1)
    convolve(w2, w1, 4, 9)
    for k in range(4):
        rows = slice(k * ROWS, (k + 1) * ROWS)
        for n, acc in enumerate((acc_a, acc_b)):
            for half in range(2):
                nat[2 * n + half, pl.ds(k, ROWS, stride=4), :] = acc[rows, half * 128 : half * 128 + 128]
    masked = feat[...].reshape(640, C).astype(F32) * present
    out_v[...] = (jnp.concatenate([nat[0], nat[1]], axis=1) + masked).astype(BF16).reshape(10, 64, C)
    upstream = cot[...].reshape(640, C).astype(F32)
    back = jnp.concatenate([nat[2], nat[3]], axis=1)
    gf_v[...] = ((upstream + back) * present).astype(BF16).reshape(10, 64, C)
    stores = [pltpu.make_async_copy(out_v, out_hbm, osem.at[0]), pltpu.make_async_copy(gf_v, gf_hbm, osem.at[1])]
    for store in stores:
        store.start()

    second_copies = []
    for h in range(2):
        to_y = [
            remote(
                sum_a.at[h, rows_at(112 * ((y + d) % 4), 112)], recv_a2.at[h, d - 1], a2s.at[h, d - 1], a2r.at[h, d - 1],
                y_peers[d - 1],
            )
            for d in (2, 1, 3)
        ]
        to_x = [
            remote(sum_b.at[h, (x + d) % 4], recv_b2.at[h, d - 1], b2s.at[h, d - 1], b2r.at[h, d - 1], x_peers[d - 1])
            for d in (2, 1, 3)
        ]
        second_copies.append((to_y, to_x))

    def end_first(h):
        for phase in (1, 2):
            for way in range(2):
                for copy in copies_of[h][phase, way]:
                    copy.wait_recv()
        for lanes, a, b, a_buf, b_buf in (
            (LOW, summed_a, direct_a, 0, 1),
            (HIGH, direct_a, summed_a, 0, 1),
        ):
            value = total(xy[slab_rows(h, x), lanes], a[h, a_buf], b[h, b_buf])
            sum_a[h, 0:432, lanes] = value.astype(BF16)
        sum_a[h, 432:448] = jnp.zeros((16, C), BF16)
        for copy in second_copies[h][0]:
            copy.start()
        for s in range(4):
            for lanes, a, b in ((LOW, summed_b, direct_b), (HIGH, direct_b, summed_b)):
                value = total(xy[part_rows(3 - h, s, y), lanes], a[h, 0, s], b[h, 1, s])
                sum_b[h, s, :, lanes] = value.astype(BF16)
        for copy in second_copies[h][1]:
            copy.start()

    stage_z = []
    for d in (4, 3, 5, 2, 6, 1, 7):
        to = (z + d) % 8
        copy = remote(zsend.at[to // 4, to % 4], zrecv.at[d - 1], zs.at[d - 1], zr.at[d - 1], z_peers[d - 1])
        stage_z.append((to, copy))

    def end_second(h):
        for copy in second_copies[h][0]:
            copy.wait_recv()
        full = total(sum_a[h, rows_at(112 * y, 112)], *[recv_a2[h, d] for d in range(3)]).astype(BF16)
        zsend[0, h], zsend[1, h] = full[:, LOW], full[:, HIGH]
        for copy in second_copies[h][1]:
            copy.wait_recv()
        full = total(sum_b[h, x], *[recv_b2[h, d] for d in range(3)]).astype(BF16)
        zsend[0, 3 - h], zsend[1, 3 - h] = full[:, LOW], full[:, HIGH]
        for to, copy in stage_z:
            outer = (to % 4 == 0) | (to % 4 == 3)

            @pl.when(outer if h == 0 else jnp.logical_not(outer))
            def _():
                copy.start()

    end_first(0)
    end_first(1)
    end_second(0)
    end_second(1)
    for _, copy in stage_z:
        copy.wait_recv()
    whole = total(zsend[z_hi, z_lo], *[zrecv[d] for d in range(7)]) * factor
    padded = jnp.concatenate([whole, jnp.zeros((16, 128), F32)], axis=0)
    fin_t[...] = padded.T.reshape(8, 16, 128)

    stage_f = []
    for d in range(1, 8):
        to = (yc + d) % 8
        stage_f.append(remote(fin_t.at[to], fin_recv.at[d - 1], fs.at[d - 1], fr.at[d - 1], f_peers[d - 1]))
    for copy in stage_f:
        copy.start()
    fin_ref[yc] = fin_t[yc]
    for d in range(1, 8):
        stage_f[d - 1].wait_recv()
    for d in range(1, 8):
        fin_ref[(yc + 8 - d) % 8] = fin_recv[d - 1]

    sent = list(first) + list(second) + [copy for _, copy in stage_z] + stage_f
    for h in range(2):
        sent += [copy for group in copies_of[h].values() for copy in group]
        sent += second_copies[h][0] + second_copies[h][1]
    for copy in sent:
        copy.wait_send()
    for store in stores:
        store.wait()

    def drain(o, carry):
        to_peer(o).wait_send()
        return carry

    lax.fori_loop(0, 27, drain, 0)


def closing(out_in, gf_in, fin, out_ref, gf_ref, g1_ref, g2_ref):
    out_ref[...] = out_in[...]
    gf_ref[...] = gf_in[...]
    for src_core, target in ((0, g1_ref), (1, g2_ref)):
        for src_y in range(4):
            size = 112 if src_y < 3 else 96
            target[:, 112 * src_y : 112 * src_y + size] = fin[src_y * 2 + src_core, :, 0:size]


def per_device(features, cotangent, neighbour_table, send_lists, block_counts, weight_one, weight_two):
    factor = 1.0 / math.sqrt(lax.axis_size("dp") * lax.axis_size("slab") * 10 * 64)
    smem = pl.BlockSpec(memory_space=pltpu.SMEM)
    vmem = pl.BlockSpec(memory_space=pltpu.VMEM)
    hbm = pl.BlockSpec(memory_space=pl.ANY)
    dma = pltpu.SemaphoreType.DMA
    big = jax.ShapeDtypeStruct((10, 64, C), BF16)
    out, gf, fin = pl.pallas_call(
        lambda *refs: kernel(factor, *refs),
        out_shape=(big, big, jax.ShapeDtypeStruct((8, 16, 128), F32)),
        in_specs=[smem, smem, vmem, hbm, hbm, hbm, hbm],
        out_specs=(hbm, hbm, vmem),
        scratch_shapes=[
            pltpu.VMEM((9, 3, C, C), BF16),
            pltpu.VMEM((9, 3, C, C), BF16),
            pltpu.VMEM((10, 64, C), BF16),
            pltpu.VMEM((10, 64, C), BF16),
            pltpu.VMEM((10, 64, C), BF16),
            pltpu.VMEM((10, 64, C), BF16),
            pltpu.VMEM((4, 640, 128), F32),
            pltpu.VMEM((10, 4, 16, 2 * C), BF16),
            pltpu.VMEM((11, 4, 16, 2 * C), BF16),
            pltpu.VMEM((2, 2, 16, 2 * C), BF16),
            pltpu.VMEM((2, 2, 16, 2 * C), BF16),
            pltpu.VMEM((10, 4, 16, 2 * C), BF16),
            pltpu.VMEM((2, 2, 16, 2 * C), BF16),
            pltpu.VMEM((2, 2, 16, 2 * C), BF16),
            pltpu.VMEM((9, 3, ROWS, REACH), BF16),
            pltpu.VMEM((9, 6, ROWS, 2 * C), BF16),
            pltpu.VMEM((640, C), F32),
            pltpu.VMEM((640, C), F32),
            pltpu.VMEM((C, 640), BF16),
            pltpu.VMEM((6912, C), BF16),
            pltpu.VMEM((6912, C), BF16),
            pltpu.VMEM((6928, C), BF16),
            pltpu.VMEM((2, 2, 432, 128), BF16),
            pltpu.VMEM((2, 2, 432, 128), BF16),
            pltpu.VMEM((2, 2, 432, 128), BF16),
            pltpu.VMEM((2, 2, 432, 128), BF16),
            pltpu.VMEM((2, 2, 4, 112, 128), BF16),
            pltpu.VMEM((2, 2, 4, 112, 128), BF16),
            pltpu.VMEM((2, 2, 4, 112, 128), BF16),
            pltpu.VMEM((2, 2, 4, 112, 128), BF16),
            pltpu.VMEM((2, 448, C), BF16),
            pltpu.VMEM((2, 4, 112, C), BF16),
            pltpu.VMEM((2, 3, 112, C), BF16),
            pltpu.VMEM((2, 3, 112, C), BF16),
            pltpu.VMEM((2, 4, 112, 128), BF16),
            pltpu.VMEM((7, 112, 128), BF16),
            pltpu.VMEM((8, 16, 128), F32),
            pltpu.VMEM((7, 16, 128), F32),
            dma((4,)),
            dma((2,)),
            dma((2, 2)),
            dma((2, 2)),
            dma((27,)),
            dma((27,)),
            dma((2, 3, 2)),
            dma((2, 3, 2)),
            dma((2, 3, 2, 4)),
            dma((2, 3, 2, 4)),
            dma((2, 3)),
            dma((2, 3)),
            dma((2, 3)),
            dma((2, 3)),
            dma((7,)),
            dma((7,)),
            dma((7,)),
            dma((7,)),
        ],
        compiler_params=pltpu.CompilerParams(
            collective_id=0, has_side_effects=True, vmem_limit_bytes=60 * 1024 * 1024
        ),
        name="step",
    )(
        block_counts,
        send_lists[0, 0],
        jnp.transpose(neighbour_table, (1, 0, 2)),
        features[0],
        cotangent[0],
        weight_one.reshape(9, 3, C, C),
        weight_two.reshape(9, 3, C, C),
    )
    piece = jax.ShapeDtypeStruct((16, 432), F32)
    out, gf, g1, g2 = pl.pallas_call(
        closing,
        out_shape=(big, big, piece, piece),
        in_specs=[vmem, vmem, vmem],
        out_specs=(vmem, vmem, vmem, vmem),
        name="closing",
    )(out, gf, fin)
    return (out[None], gf[None], g1.T, g2.T)


def solution(mesh):
    in_specs = (
        P("dp", "slab", None, None),
        P("dp", "slab", None, None),
        P("dp", "slab", None),
        P("dp", "slab", None, None),
        P("dp", "slab"),
        P(),
        P(),
    )
    out_specs = (
        P("dp", "slab", None, None),
        P("dp", "slab", None, None),
        P("slab", "dp"),
        P("slab", "dp"),
    )
    return jax.shard_map(
        per_device, mesh=mesh, in_specs=in_specs, out_specs=out_specs, check_vma=False
    )
```

time: 89.8 us -> 71.4 us (0.80)
  the two profiles are of different devices: /device:TPU:1 before, /device:TPU:33 now
where the time goes in v1:
time: 71.4 us; the launch traced here: 71.2 us
  Pallas kernels  69.9 us (98%)
  between operations  1.29 us (2%)
    pallas_call x1, Pallas kernels, per_device(): pl.pallas_call(lambda *refs: kernel(factor, *refs), out_shape=(big, big,...  68 us
    pallas_call x1, Pallas kernels, per_device(): pl.pallas_call(closing, out_shape=(big, big, piece, piece), in_specs=[vme...  1.94 us

profile of v1, /device:TPU:33, one launch (start us, length us, event | category | flops | bytes accessed | tf_op | source)
XLA Modules:
  0.0 71.2 jit_solution(11141852985495868554)
XLA Ops:
  1.3 68.0 %step.1 = (bf16[10,64,256]{2,1,0:T(8,128)(2,1)}, bf16[10,64,256]{2,1,0:T(8,128)(2,1)}, f32[8,16,128]{2,1,0:T(8,128)}) custom-call(s32[1,1]{1,0:T(1,128)S(6)} %copy.11.refs_0_, s32[2,2]{1,0:T(2,128)} %bitcast.15, s32[10,1,27]{2,1,0:T(1,128)} %bitcast.14, bf16[10,64,256]{2,1,0:T(8,128)(2,1)} %bitcast.12, bf16[10,64,256]{2,1,0:T(8,128)(2,1)} %bitcast.13, ...), custom_call_target="tpu_custom_call" | custom-call | tf_op jit(solution)/shard_map/step/pallas_call | solution.py:437
  69.3 1.9 %closing.1 = (bf16[10,64,256]{2,1,0:T(8,128)(2,1)}, bf16[10,64,256]{2,1,0:T(8,128)(2,1)}, f32[16,432]{1,0:T(8,128)}, f32[16,432]{1,0:T(8,128)}) custom-call(bf16[10,64,256]{2,1,0:T(8,128)(2,1)} %get-tuple-element.11.out_in, bf16[10,64,256]{2,1,0:T(8,128)(2,1)} %get-tuple-element.12.gf_in, f32[8,16,128]{2,1,0:T(8,128)} %get-tuple-element.13.fin), custom_call_target="tpu_custom_call" | custom-call | tf_op jit(solution)/shard_map/closing/pallas_call | solution.py:514

commit v2 on v1

--- a/solution.py
+++ b/solution.py
@@ -26,7 +26,7 @@
     counts, lists, table_ref, feat_hbm, cot_hbm, w1_hbm, w2_hbm,
     out_hbm, gf_hbm, fin_ref,
     w1, w2, feat, cot, out_v, gf_v, nat, t_own, t_ext, pack, hrecv, t_own2, pack2, hrecv2, sel, win, acc_a, acc_b,
-    hid_t, psend, precv, xy, relay_a, direct_a, summed_a, stage_a, relay_b, direct_b, summed_b, stage_b,
+    hid_t, mine, precv, relay_a, direct_a, summed_a, stage_a, relay_b, direct_b, summed_b, stage_b,
     sum_a, sum_b, recv_a2, recv_b2, zsend, zrecv, fin_t, fin_recv,
     lsem, osem, hs, hr, ps, pr, as_, ar, bs, br, a2s, a2r, b2s, b2r, zs, zr, fs, fr,
 ):
@@ -132,7 +132,7 @@
                         block = value if block is None else jnp.where(cond, value, block)
                 block = block.astype(jnp.int32)
                 source = jnp.where(block < 10, block * 16 + spot, 160 + (block - 10) * 4 + spot_j)
-                sel[dx * 3 + dy, bz] = jnp.where(lane == source, 1.0, 0.0).astype(BF16)
+                sel[dx, bz, dy * ROWS : dy * ROWS + ROWS] = jnp.where(lane == source, 1.0, 0.0).astype(BF16)
 
     def finish_halo(copies, received, ext):
         for copy in copies:
@@ -141,87 +141,82 @@
         for k in range(4):
             ext[10, k] = jnp.concatenate([plane[4 * k : 4 * k + 4] for plane in planes], axis=0).astype(BF16)
 
-    def build(ext):
-        def one(g, carry):
-            for spot in range(6):
-                k = (spot + 3) % 4
-                bz = 0 if spot == 0 else 2 if spot == 5 else 1
-                win[g, spot] = dot(sel[g, bz], ext[:, k].reshape(REACH, 2 * C)).astype(BF16)
+    def build(ext, dx):
+        for k in range(4):
+            parts = [(k + 1, 1)] + ([(5, 2)] if k == 0 else [(0, 0)] if k == 3 else [])
+            left = jnp.concatenate([sel[dx, bz] for _, bz in parts], axis=0)
+            rows = dot(left, ext[:, k].reshape(REACH, 2 * C)).astype(BF16)
+            for n, (spot, _) in enumerate(parts):
+                for dy in range(3):
+                    at = (3 * n + dy) * ROWS
+                    win[dx * 3 + dy, spot] = rows[at : at + ROWS]
+
+    def view(g, dz, low):
+        return win[g, dz : dz + 4, :, low : low + C].reshape(640, C)
+
+    def forward(g, w):
+        left = jnp.concatenate([view(g, dz, 0) for dz in range(3)], axis=1)
+        acc_a[...] += dot(left, w[g].reshape(3 * C, C))
+
+    def backward(g, w):
+        left = jnp.concatenate([view(g, dz, C) for dz in range(3)], axis=1)
+        right = jnp.concatenate([w[8 - g, 2 - dz] for dz in range(3)], axis=1)
+        acc_b[...] += dot(left, right, NT)
+
+    def each(start, end, step):
+        def one(n, carry):
+            step(n)
             return carry
 
-        lax.fori_loop(0, 9, one, 0)
-
-    def view(g, dz, low):
-        return win[g, pl.ds(dz, 4), :, low : low + C].reshape(640, C)
-
-    def convolve(w_fwd, w_bwd, start, end):
-        if start == 0:
-            acc_a[...] = jnp.zeros_like(acc_a)
-            acc_b[...] = jnp.zeros_like(acc_b)
-
-        def one(g, carry):
-            left = jnp.concatenate([view(g, dz, 0) for dz in range(3)], axis=1)
-            acc_a[...] += dot(left, w_fwd[g].reshape(3 * C, C))
-            left = jnp.concatenate([view(g, dz, C) for dz in range(3)], axis=1)
-            right = jnp.concatenate([w_bwd[8 - g, 2 - dz] for dz in range(3)], axis=1)
-            acc_b[...] += dot(left, right, NT)
-            return carry
-
         lax.fori_loop(start, end, one, 0)
 
+    def sides(step):
+        each(0, 6, lambda n: step(jnp.where(n < 3, n, n + 3)))
+
+    acc_a[...] = jnp.zeros_like(acc_a)
+    acc_b[...] = jnp.zeros_like(acc_b)
+    for k in range(4):
+        t_ext[10, k] = jnp.zeros((16, 2 * C), BF16)
+    build(t_ext, 1)
+    loads[2].wait()
+    each(3, 6, lambda g: forward(g, w1))
+    loads[3].wait()
+    each(3, 6, lambda g: backward(g, w2))
     finish_halo(first, hrecv, t_ext)
-    build(t_ext)
-    loads[2].wait()
-    loads[3].wait()
-    convolve(w1, w2, 0, 9)
+    each(0, 2, lambda n: build(t_ext, 2 * n))
+    sides(lambda g: forward(g, w1))
 
     hidden = jnp.maximum(acc_a[...], 0.0)
-    rounded = hidden.astype(BF16)
-    grad_hidden = jnp.where(rounded > 0, acc_b[...].astype(BF16), jnp.zeros((), BF16))
     hid_t[...] = hidden.T.astype(BF16)
+    hidden = hidden.astype(BF16)
     for k in range(4):
-        rows = slice(k * ROWS, (k + 1) * ROWS)
-        t_own2[:, k, :, 0:C] = rounded[rows].reshape(10, 16, C)
-        t_own2[:, k, :, C:] = grad_hidden[rows].reshape(10, 16, C)
-        t_ext[0:10, k, :, 0:C] = rounded[rows].reshape(10, 16, C)
-        t_ext[0:10, k, :, C:] = grad_hidden[rows].reshape(10, 16, C)
-    pack_edges(t_own2, pack2)
-    second = halo(pack2, hrecv2, 1)
-    for copy in second:
-        copy.start()
-
-    def block_of(o):
-        return pl.ds(pl.multiple_of(o * C, C), C)
-
-    def to_peer(o):
-        return remote(psend.at[block_of(o)], precv.at[block_of(o)], ps.at[o], pr.at[o], peer)
-
-    gh_rows = jnp.concatenate([t_own2[:, k, :, C:].reshape(ROWS, C) for k in range(4)], axis=0)
-
-    def grad_at(o):
-        one = dot(view(o // 3, o % 3, 0), gh_rows, TN)
-        two = dot(hid_t[...], view(8 - o // 3, 2 - o % 3, C))
-        xy[block_of(o)] = jnp.where(core == 0, one, two).astype(BF16)
-        psend[block_of(o)] = jnp.where(core == 0, two, one).astype(BF16)
-        to_peer(o).start()
-
-    def grads(n, carry):
-        grad_at(n)
-        grad_at(26 - n)
-        return carry
-
-    def join(o):
-        to_peer(o).wait_recv()
-        xy[block_of(o)] = (xy[block_of(o)].astype(F32) + precv[block_of(o)].astype(F32)).astype(BF16)
-
-    def join_ends(n, carry):
-        join(n)
-        join(26 - n)
-        return carry
-
-    def join_middle(n, carry):
-        join(n)
-        return carry
+        rows = hidden[k * ROWS : (k + 1) * ROWS].reshape(10, 16, C)
+        t_own2[:, k, :, 0:C] = rows
+        t_ext[0:10, k, :, 0:C] = rows
+
+    def three(g):
+        return pl.ds(pl.multiple_of(g * 768, 768), 768)
+
+    def to_peer(g):
+        return remote(mine.at[1, three(g)], precv.at[three(g)], ps.at[g], pr.at[g], peer)
+
+    def grad_two_at(g):
+        for dz in range(3):
+            value = dot(hid_t[...], view(8 - g, 2 - dz, C))
+            mine[1 - core, pl.ds(g * 768 + dz * C, C)] = value.astype(BF16)
+
+    def grad_one_at(g):
+        gh_rows = jnp.concatenate([t_own2[:, k, :, C:].reshape(ROWS, C) for k in range(4)], axis=0)
+        left = jnp.concatenate([view(g, dz, 0) for dz in range(3)], axis=1)
+        mine[core, three(g)] = dot(left, gh_rows, TN).astype(BF16)
+
+    def join(g):
+        to_peer(g).wait_recv()
+        for n in range(3):
+            at = pl.ds(g * 768 + n * C, C)
+            xy[at] = (xy[at].astype(F32) + precv[at].astype(F32)).astype(BF16)
+
+    xy = mine.at[0]
 
     def rows_at(start, size):
         return pl.ds(pl.multiple_of(start, 16), size)
@@ -268,11 +263,23 @@
 
     copies_of = [first_copies(0), first_copies(1)]
 
-    def start_first(h):
-        for phase in range(2):
-            a0, b0 = copies_of[h][phase, 0], copies_of[h][phase, 1]
-            for copy in [c for pair in zip(a0, b0) for c in pair]:
-                copy.start()
+    def start_slab(s):
+        h = min(s // 4, 3 - s // 4)
+        for way in range(2):
+            if s < 8:
+                owner = next_x if way == 0 else last_x
+
+                @pl.when(far_x == s % 4)
+                def _():
+                    copies_of[h][0, way][0].start()
+
+                @pl.when(owner == s % 4)
+                def _():
+                    copies_of[h][1, way][0].start()
+
+            else:
+                for phase in range(2):
+                    copies_of[h][phase, way][1 + s % 4].start()
 
     def total(*parts):
         value = parts[0].astype(F32)
@@ -291,36 +298,6 @@
                 stage_b[h, way, s] = total(own, relay_b[h, way, s]).astype(BF16)
             for copy in copies_of[h][2, way]:
                 copy.start()
-
-    lax.fori_loop(0, 7, grads, 0)
-    xy[6912:6928] = jnp.zeros((16, C), BF16)
-    lax.fori_loop(7, 9, grads, 0)
-    lax.fori_loop(0, 7, join_ends, 0)
-    start_first(0)
-    lax.fori_loop(9, 13, grads, 0)
-    grad_at(13)
-    lax.fori_loop(7, 20, join_middle, 0)
-    start_first(1)
-
-    finish_halo(second, hrecv2, t_ext)
-    build(t_ext)
-    pass_on(0)
-    convolve(w2, w1, 0, 4)
-    pass_on(1)
-    convolve(w2, w1, 4, 9)
-    for k in range(4):
-        rows = slice(k * ROWS, (k + 1) * ROWS)
-        for n, acc in enumerate((acc_a, acc_b)):
-            for half in range(2):
-                nat[2 * n + half, pl.ds(k, ROWS, stride=4), :] = acc[rows, half * 128 : half * 128 + 128]
-    masked = feat[...].reshape(640, C).astype(F32) * present
-    out_v[...] = (jnp.concatenate([nat[0], nat[1]], axis=1) + masked).astype(BF16).reshape(10, 64, C)
-    upstream = cot[...].reshape(640, C).astype(F32)
-    back = jnp.concatenate([nat[2], nat[3]], axis=1)
-    gf_v[...] = ((upstream + back) * present).astype(BF16).reshape(10, 64, C)
-    stores = [pltpu.make_async_copy(out_v, out_hbm, osem.at[0]), pltpu.make_async_copy(gf_v, gf_hbm, osem.at[1])]
-    for store in stores:
-        store.start()
 
     second_copies = []
     for h in range(2):
@@ -380,10 +357,76 @@
             def _():
                 copy.start()
 
-    end_first(0)
-    end_first(1)
-    end_second(0)
-    end_second(1)
+    def on(which, *steps):
+        @pl.when(core == which)
+        def _():
+            for step, arg in steps:
+                step(arg)
+
+    READY = ((0, 15), (1, 14, 2, 13), (3, 12, 4, 11), (5, 10, 6, 9), (7, 8))
+
+    def gradients(at, keeper, between):
+        def finish(n):
+            for g in (n, 8 - n) if n < 4 else (4,):
+                join(g)
+            for s in READY[n]:
+                start_slab(s)
+
+        def send(g):
+            to_peer(g).start()
+
+        for n in range(5):
+            for g in (n, 8 - n) if n < 4 else (4,):
+                at(g)
+                on(1 - keeper, (send, g))
+            if n > 0:
+                on(keeper, (finish, n - 1))
+            between(n)
+        on(keeper, (finish, 4))
+
+    xy[6912:6928] = jnp.zeros((16, C), BF16)
+    gradients(grad_two_at, 1, lambda n: None)
+
+    sides(lambda g: backward(g, w2))
+    grad_hidden = jnp.where(hidden > 0, acc_b[...].astype(BF16), jnp.zeros((), BF16))
+    for k in range(4):
+        rows = grad_hidden[k * ROWS : (k + 1) * ROWS].reshape(10, 16, C)
+        t_own2[:, k, :, C:] = rows
+        t_ext[0:10, k, :, C:] = rows
+    pack_edges(t_own2, pack2)
+    second = halo(pack2, hrecv2, 1)
+    for copy in second:
+        copy.start()
+    on(1, (pass_on, 0))
+
+    gradients(grad_one_at, 0, lambda n: on(1, (pass_on, 1)) if n == 2 else None)
+
+    finish_halo(second, hrecv2, t_ext)
+    each(0, 3, lambda dx: build(t_ext, dx))
+    on(0, (pass_on, 0))
+    on(1, (end_first, 0))
+    acc_a[...] = jnp.zeros_like(acc_a)
+    acc_b[...] = jnp.zeros_like(acc_b)
+    each(0, 9, lambda g: forward(g, w2))
+    on(0, (pass_on, 1))
+    on(1, (end_first, 1), (end_second, 0))
+    each(0, 9, lambda g: backward(g, w1))
+    on(1, (end_second, 1))
+    for k in range(4):
+        rows = slice(k * ROWS, (k + 1) * ROWS)
+        for n, acc in enumerate((acc_a, acc_b)):
+            for half in range(2):
+                nat[2 * n + half, pl.ds(k, ROWS, stride=4), :] = acc[rows, half * 128 : half * 128 + 128]
+    masked = feat[...].reshape(640, C).astype(F32) * present
+    out_v[...] = (jnp.concatenate([nat[0], nat[1]], axis=1) + masked).astype(BF16).reshape(10, 64, C)
+    upstream = cot[...].reshape(640, C).astype(F32)
+    back = jnp.concatenate([nat[2], nat[3]], axis=1)
+    gf_v[...] = ((upstream + back) * present).astype(BF16).reshape(10, 64, C)
+    stores = [pltpu.make_async_copy(out_v, out_hbm, osem.at[0]), pltpu.make_async_copy(gf_v, gf_hbm, osem.at[1])]
+    for store in stores:
+        store.start()
+
+    on(0, (end_first, 0), (end_first, 1), (end_second, 0), (end_second, 1))
     for _, copy in stage_z:
         copy.wait_recv()
     whole = total(zsend[z_hi, z_lo], *[zrecv[d] for d in range(7)]) * factor
@@ -411,11 +454,7 @@
     for store in stores:
         store.wait()
 
-    def drain(o, carry):
-        to_peer(o).wait_send()
-        return carry
-
-    lax.fori_loop(0, 27, drain, 0)
+    each(0, 9, lambda g: to_peer(g).wait_send())
 
 
 def closing(out_in, gf_in, fin, out_ref, gf_ref, g1_ref, g2_ref):
@@ -454,14 +493,13 @@
             pltpu.VMEM((10, 4, 16, 2 * C), BF16),
             pltpu.VMEM((2, 2, 16, 2 * C), BF16),
             pltpu.VMEM((2, 2, 16, 2 * C), BF16),
-            pltpu.VMEM((9, 3, ROWS, REACH), BF16),
+            pltpu.VMEM((3, 3, 3 * ROWS, REACH), BF16),
             pltpu.VMEM((9, 6, ROWS, 2 * C), BF16),
             pltpu.VMEM((640, C), F32),
             pltpu.VMEM((640, C), F32),
             pltpu.VMEM((C, 640), BF16),
+            pltpu.VMEM((2, 6928, C), BF16),
             pltpu.VMEM((6912, C), BF16),
-            pltpu.VMEM((6912, C), BF16),
-            pltpu.VMEM((6928, C), BF16),
             pltpu.VMEM((2, 2, 432, 128), BF16),
             pltpu.VMEM((2, 2, 432, 128), BF16),
             pltpu.VMEM((2, 2, 432, 128), BF16),
@@ -482,8 +520,8 @@
             dma((2,)),
             dma((2, 2)),
             dma((2, 2)),
-            dma((27,)),
-            dma((27,)),
+            dma((9,)),
+            dma((9,)),
             dma((2, 3, 2)),
             dma((2, 3, 2)),
             dma((2, 3, 2, 4)),

time: 71.4 us -> 69.8 us (0.978)
  the two profiles are of different devices: /device:TPU:33 before, /device:TPU:1 now
where the time goes in v2:
time: 69.8 us; the launch traced here: 69.7 us
  Pallas kernels  68.4 us (98%)
  between operations  1.29 us (2%)
    pallas_call x1, Pallas kernels, per_device(): pl.pallas_call(lambda *refs: kernel(factor, *refs), out_shape=(big, big,...  66.4 us
    pallas_call x1, Pallas kernels, per_device(): pl.pallas_call(closing, out_shape=(big, big, piece, piece), in_specs=[vme...  1.94 us

profile of v2, /device:TPU:1, one launch (start us, length us, event | category | flops | bytes accessed | tf_op | source)
XLA Modules:
  0.0 69.7 jit_solution(6792558155472372186)
XLA Ops:
  1.3 66.4 %step.1 = (bf16[10,64,256]{2,1,0:T(8,128)(2,1)}, bf16[10,64,256]{2,1,0:T(8,128)(2,1)}, f32[8,16,128]{2,1,0:T(8,128)}) custom-call(s32[1,1]{1,0:T(1,128)S(6)} %copy.11.refs_0_, s32[2,2]{1,0:T(2,128)} %bitcast.15, s32[10,1,27]{2,1,0:T(1,128)} %bitcast.14, bf16[10,64,256]{2,1,0:T(8,128)(2,1)} %bitcast.12, bf16[10,64,256]{2,1,0:T(8,128)(2,1)} %bitcast.13, ...), custom_call_target="tpu_custom_call" | custom-call | tf_op jit(solution)/shard_map/step/pallas_call | solution.py:476
  67.7 1.9 %closing.1 = (bf16[10,64,256]{2,1,0:T(8,128)(2,1)}, bf16[10,64,256]{2,1,0:T(8,128)(2,1)}, f32[16,432]{1,0:T(8,128)}, f32[16,432]{1,0:T(8,128)}) custom-call(bf16[10,64,256]{2,1,0:T(8,128)(2,1)} %get-tuple-element.11.out_in, bf16[10,64,256]{2,1,0:T(8,128)(2,1)} %get-tuple-element.12.gf_in, f32[8,16,128]{2,1,0:T(8,128)} %get-tuple-element.13.fin), custom_call_target="tpu_custom_call" | custom-call | tf_op jit(solution)/shard_map/closing/pallas_call | solution.py:552

commit v3 on v2

--- a/solution.py
+++ b/solution.py
@@ -26,7 +26,7 @@
     counts, lists, table_ref, feat_hbm, cot_hbm, w1_hbm, w2_hbm,
     out_hbm, gf_hbm, fin_ref,
     w1, w2, feat, cot, out_v, gf_v, nat, t_own, t_ext, pack, hrecv, t_own2, pack2, hrecv2, sel, win, acc_a, acc_b,
-    hid_t, mine, precv, relay_a, direct_a, summed_a, stage_a, relay_b, direct_b, summed_b, stage_b,
+    hid_t, gh_t, mine, precv, relay_a, direct_a, summed_a, stage_a, relay_b, direct_b, summed_b, stage_b,
     sum_a, sum_b, recv_a2, recv_b2, zsend, zrecv, fin_t, fin_recv,
     lsem, osem, hs, hr, ps, pr, as_, ar, bs, br, a2s, a2r, b2s, b2r, zs, zr, fs, fr,
 ):
@@ -154,14 +154,16 @@
     def view(g, dz, low):
         return win[g, dz : dz + 4, :, low : low + C].reshape(640, C)
 
-    def forward(g, w):
-        left = jnp.concatenate([view(g, dz, 0) for dz in range(3)], axis=1)
-        acc_a[...] += dot(left, w[g].reshape(3 * C, C))
-
-    def backward(g, w):
-        left = jnp.concatenate([view(g, dz, C) for dz in range(3)], axis=1)
-        right = jnp.concatenate([w[8 - g, 2 - dz] for dz in range(3)], axis=1)
-        acc_b[...] += dot(left, right, NT)
+    def views(gs, low):
+        return jnp.concatenate([view(g, dz, low) for g in gs for dz in range(3)], axis=1)
+
+    def forward(gs, w):
+        right = jnp.concatenate([w[g].reshape(3 * C, C) for g in gs], axis=0)
+        acc_a[...] += dot(views(gs, 0), right)
+
+    def backward(gs, w):
+        right = jnp.concatenate([w[8 - g, 2 - dz] for g in gs for dz in range(3)], axis=1)
+        acc_b[...] += dot(views(gs, C), right, NT)
 
     def each(start, end, step):
         def one(n, carry):
@@ -171,7 +173,7 @@
         lax.fori_loop(start, end, one, 0)
 
     def sides(step):
-        each(0, 6, lambda n: step(jnp.where(n < 3, n, n + 3)))
+        each(0, 3, lambda n: step((n, n + 6)))
 
     acc_a[...] = jnp.zeros_like(acc_a)
     acc_b[...] = jnp.zeros_like(acc_b)
@@ -179,12 +181,12 @@
         t_ext[10, k] = jnp.zeros((16, 2 * C), BF16)
     build(t_ext, 1)
     loads[2].wait()
-    each(3, 6, lambda g: forward(g, w1))
+    forward((3, 4, 5), w1)
     loads[3].wait()
-    each(3, 6, lambda g: backward(g, w2))
+    backward((3, 4, 5), w2)
     finish_halo(first, hrecv, t_ext)
     each(0, 2, lambda n: build(t_ext, 2 * n))
-    sides(lambda g: forward(g, w1))
+    sides(lambda gs: forward(gs, w1))
 
     hidden = jnp.maximum(acc_a[...], 0.0)
     hid_t[...] = hidden.T.astype(BF16)
@@ -201,14 +203,12 @@
         return remote(mine.at[1, three(g)], precv.at[three(g)], ps.at[g], pr.at[g], peer)
 
     def grad_two_at(g):
+        value = dot(hid_t[...], jnp.concatenate([view(8 - g, 2 - dz, C) for dz in range(3)], axis=1)).astype(BF16)
         for dz in range(3):
-            value = dot(hid_t[...], view(8 - g, 2 - dz, C))
-            mine[1 - core, pl.ds(g * 768 + dz * C, C)] = value.astype(BF16)
+            mine[1 - core, pl.ds(g * 768 + dz * C, C)] = value[:, dz * C : dz * C + C]
 
     def grad_one_at(g):
-        gh_rows = jnp.concatenate([t_own2[:, k, :, C:].reshape(ROWS, C) for k in range(4)], axis=0)
-        left = jnp.concatenate([view(g, dz, 0) for dz in range(3)], axis=1)
-        mine[core, three(g)] = dot(left, gh_rows, TN).astype(BF16)
+        mine[core, three(g)] = dot(gh_t[...], views((g,), 0)).astype(BF16).T
 
     def join(g):
         to_peer(g).wait_recv()
@@ -376,9 +376,10 @@
             to_peer(g).start()
 
         for n in range(5):
-            for g in (n, 8 - n) if n < 4 else (4,):
+            gs = (n, 8 - n) if n < 4 else (4,)
+            for g in gs:
                 at(g)
-                on(1 - keeper, (send, g))
+            on(1 - keeper, *[(send, g) for g in gs])
             if n > 0:
                 on(keeper, (finish, n - 1))
             between(n)
@@ -387,8 +388,9 @@
     xy[6912:6928] = jnp.zeros((16, C), BF16)
     gradients(grad_two_at, 1, lambda n: None)
 
-    sides(lambda g: backward(g, w2))
+    sides(lambda gs: backward(gs, w2))
     grad_hidden = jnp.where(hidden > 0, acc_b[...].astype(BF16), jnp.zeros((), BF16))
+    gh_t[...] = grad_hidden.T
     for k in range(4):
         rows = grad_hidden[k * ROWS : (k + 1) * ROWS].reshape(10, 16, C)
         t_own2[:, k, :, C:] = rows
@@ -407,10 +409,10 @@
     on(1, (end_first, 0))
     acc_a[...] = jnp.zeros_like(acc_a)
     acc_b[...] = jnp.zeros_like(acc_b)
-    each(0, 9, lambda g: forward(g, w2))
+    each(0, 3, lambda n: forward((3 * n, 3 * n + 1, 3 * n + 2), w2))
     on(0, (pass_on, 1))
     on(1, (end_first, 1), (end_second, 0))
-    each(0, 9, lambda g: backward(g, w1))
+    each(0, 3, lambda n: backward((3 * n, 3 * n + 1, 3 * n + 2), w1))
     on(1, (end_second, 1))
     for k in range(4):
         rows = slice(k * ROWS, (k + 1) * ROWS)
@@ -497,6 +499,7 @@
             pltpu.VMEM((9, 6, ROWS, 2 * C), BF16),
             pltpu.VMEM((640, C), F32),
             pltpu.VMEM((640, C), F32),
+            pltpu.VMEM((C, 640), BF16),
             pltpu.VMEM((C, 640), BF16),
             pltpu.VMEM((2, 6928, C), BF16),
             pltpu.VMEM((6912, C), BF16),

time: 69.8 us -> 65.6 us (0.940)
  Pallas kernels: 68.4 us -> 64.2 us
    pallas_call x1, Pallas kernels: 66.4 us -> 62.3 us  [per_device(): pl.pallas_call(lambda *refs: kernel(factor, *refs), out_shape=(big, big,...]
where the time goes in v3:
time: 65.6 us; the launch traced here: 65.5 us
  Pallas kernels  64.2 us (98%)
  between operations  1.29 us (2%)
    pallas_call x1, Pallas kernels, per_device(): pl.pallas_call(lambda *refs: kernel(factor, *refs), out_shape=(big, big,...  62.3 us
    pallas_call x1, Pallas kernels, per_device(): pl.pallas_call(closing, out_shape=(big, big, piece, piece), in_specs=[vme...  1.94 us

profile of v3, /device:TPU:1, one launch (start us, length us, event | category | flops | bytes accessed | tf_op | source)
XLA Modules:
  0.0 65.5 jit_solution(1554692694667277167)
XLA Ops:
  1.3 62.3 %step.1 = (bf16[10,64,256]{2,1,0:T(8,128)(2,1)}, bf16[10,64,256]{2,1,0:T(8,128)(2,1)}, f32[8,16,128]{2,1,0:T(8,128)}) custom-call(s32[1,1]{1,0:T(1,128)S(6)} %copy.11.refs_0_, s32[2,2]{1,0:T(2,128)} %bitcast.15, s32[10,1,27]{2,1,0:T(1,128)} %bitcast.14, bf16[10,64,256]{2,1,0:T(8,128)(2,1)} %bitcast.12, bf16[10,64,256]{2,1,0:T(8,128)(2,1)} %bitcast.13, ...), custom_call_target="tpu_custom_call" | custom-call | tf_op jit(solution)/shard_map/step/pallas_call | solution.py:478
  63.5 1.9 %closing.1 = (bf16[10,64,256]{2,1,0:T(8,128)(2,1)}, bf16[10,64,256]{2,1,0:T(8,128)(2,1)}, f32[16,432]{1,0:T(8,128)}, f32[16,432]{1,0:T(8,128)}) custom-call(bf16[10,64,256]{2,1,0:T(8,128)(2,1)} %get-tuple-element.11.out_in, bf16[10,64,256]{2,1,0:T(8,128)(2,1)} %get-tuple-element.12.gf_in, f32[8,16,128]{2,1,0:T(8,128)} %get-tuple-element.13.fin), custom_call_target="tpu_custom_call" | custom-call | tf_op jit(solution)/shard_map/closing/pallas_call | solution.py:555

commit v4 on v3

--- a/solution.py
+++ b/solution.py
@@ -106,33 +106,37 @@
         copy.start()
 
     r = lax.broadcasted_iota(jnp.int32, (ROWS, 1), 0)
-    spread = (r // 16 == lax.broadcasted_iota(jnp.int32, (ROWS, 10), 1)).astype(F32)
-    rows_of = dot(spread, table_ref[...].reshape(10, 27).astype(F32))
-    i_of, j_of = r // 4 % 4, r % 4
+    spread = (r // 16 == lax.broadcasted_iota(jnp.int32, (ROWS, 10), 1)).astype(BF16)
+    rows_of = dot(spread, table_ref[...].reshape(10, 27).astype(BF16)).astype(BF16)
+    named = lax.broadcasted_iota(jnp.int32, (27, 27), 0)
+
+    def step_of(shape):
+        m = lax.broadcasted_iota(jnp.int32, shape, 1)
+        return m // 9, m // 3 % 3, m % 3
+
+    step_x, step_y, step_z = step_of((27, 27))
+    low = (jnp.minimum(step_x, 1), jnp.minimum(step_y, 1))
+    high = (jnp.maximum(step_x, 1), jnp.maximum(step_y, 1))
+
+    def blocks(bx, by):
+        return dot(rows_of, (named == 9 * bx + 3 * by + step_z).astype(BF16))
+
+    step_x, step_y, _ = step_of((ROWS, 27))
+    at_x, at_y = r // 4 % 4 + step_x - 1, r % 4 + step_y - 1
+    first_x = at_x < jnp.where(step_x == 0, 0, 4)
+    first_y = at_y < jnp.where(step_y == 0, 0, 4)
+    block = jnp.where(
+        first_x,
+        jnp.where(first_y, blocks(low[0], low[1]), blocks(low[0], high[1])),
+        jnp.where(first_y, blocks(high[0], low[1]), blocks(high[0], high[1])),
+    ).astype(jnp.int32)
+    spot_y = (at_y + 4) % 4
+    from_own = block * 16 + (at_x + 4) % 4 * 4 + spot_y
+    source = jnp.where(block < 10, from_own, 160 + (block - 10) * 4 + spot_y)
     lane = lax.broadcasted_iota(jnp.int32, (ROWS, REACH), 1)
-
-    def options(position, step):
-        if step == 0:
-            return [(0, position == 0), (1, position > 0)]
-        if step == 1:
-            return [(1, None)]
-        return [(1, position < 3), (2, position == 3)]
-
-    for dx in range(3):
-        for dy in range(3):
-            spot_j = (j_of + dy + 3) % 4
-            spot = (i_of + dx + 3) % 4 * 4 + spot_j
-            for bz in range(3):
-                block = None
-                for bx, cond_x in options(i_of, dx):
-                    for by, cond_y in options(j_of, dy):
-                        n = 9 * bx + 3 * by + bz
-                        value = rows_of[:, n : n + 1]
-                        cond = cond_x if cond_y is None else cond_y if cond_x is None else cond_x & cond_y
-                        block = value if block is None else jnp.where(cond, value, block)
-                block = block.astype(jnp.int32)
-                source = jnp.where(block < 10, block * 16 + spot, 160 + (block - 10) * 4 + spot_j)
-                sel[dx, bz, dy * ROWS : dy * ROWS + ROWS] = jnp.where(lane == source, 1.0, 0.0).astype(BF16)
+    for m in range(27):
+        chosen = jnp.where(lane == source[:, m : m + 1], 1.0, 0.0).astype(BF16)
+        sel[m // 9, m % 3, m // 3 % 3 * ROWS : (m // 3 % 3 + 1) * ROWS] = chosen
 
     def finish_halo(copies, received, ext):
         for copy in copies:
@@ -404,15 +408,19 @@
     gradients(grad_one_at, 0, lambda n: on(1, (pass_on, 1)) if n == 2 else None)
 
     finish_halo(second, hrecv2, t_ext)
-    each(0, 3, lambda dx: build(t_ext, dx))
+    build(t_ext, 0)
     on(0, (pass_on, 0))
     on(1, (end_first, 0))
+    each(1, 3, lambda dx: build(t_ext, dx))
+    on(0, (pass_on, 1))
+    on(1, (end_first, 1))
     acc_a[...] = jnp.zeros_like(acc_a)
     acc_b[...] = jnp.zeros_like(acc_b)
     each(0, 3, lambda n: forward((3 * n, 3 * n + 1, 3 * n + 2), w2))
-    on(0, (pass_on, 1))
-    on(1, (end_first, 1), (end_second, 0))
+    on(0, (end_first, 0))
+    on(1, (end_second, 0))
     each(0, 3, lambda n: backward((3 * n, 3 * n + 1, 3 * n + 2), w1))
+    on(0, (end_first, 1))
     on(1, (end_second, 1))
     for k in range(4):
         rows = slice(k * ROWS, (k + 1) * ROWS)
@@ -428,7 +436,7 @@
     for store in stores:
         store.start()
 
-    on(0, (end_first, 0), (end_first, 1), (end_second, 0), (end_second, 1))
+    on(0, (end_second, 0), (end_second, 1))
     for _, copy in stage_z:
         copy.wait_recv()
     whole = total(zsend[z_hi, z_lo], *[zrecv[d] for d in range(7)]) * factor

time: 65.6 us -> 67.1 us (1.023); the launches traced: 65.5 us -> 65.8 us
  no operation moved by 1% of the time
where the time goes in v4:
time: 67.1 us; the launch traced here: 65.8 us
  Pallas kernels  64.5 us (96%)
  between operations  1.29 us (2%)
    pallas_call x1, Pallas kernels, per_device(): pl.pallas_call(lambda *refs: kernel(factor, *refs), out_shape=(big, big,...  62.5 us
    pallas_call x1, Pallas kernels, per_device(): pl.pallas_call(closing, out_shape=(big, big, piece, piece), in_specs=[vme...  1.94 us

profile of v4, /device:TPU:1, one launch (start us, length us, event | category | flops | bytes accessed | tf_op | source)
XLA Modules:
  0.0 65.8 jit_solution(13603778057450032671)
XLA Ops:
  1.3 62.5 %step.1 = (bf16[10,64,256]{2,1,0:T(8,128)(2,1)}, bf16[10,64,256]{2,1,0:T(8,128)(2,1)}, f32[8,16,128]{2,1,0:T(8,128)}) custom-call(s32[1,1]{1,0:T(1,128)S(6)} %copy.11.refs_0_, s32[2,2]{1,0:T(2,128)} %bitcast.15, s32[10,1,27]{2,1,0:T(1,128)} %bitcast.14, bf16[10,64,256]{2,1,0:T(8,128)(2,1)} %bitcast.12, bf16[10,64,256]{2,1,0:T(8,128)(2,1)} %bitcast.13, ...), custom_call_target="tpu_custom_call" | custom-call | tf_op jit(solution)/shard_map/step/pallas_call | solution.py:486
  63.8 1.9 %closing.1 = (bf16[10,64,256]{2,1,0:T(8,128)(2,1)}, bf16[10,64,256]{2,1,0:T(8,128)(2,1)}, f32[16,432]{1,0:T(8,128)}, f32[16,432]{1,0:T(8,128)}) custom-call(bf16[10,64,256]{2,1,0:T(8,128)(2,1)} %get-tuple-element.11.out_in, bf16[10,64,256]{2,1,0:T(8,128)(2,1)} %get-tuple-element.12.gf_in, f32[8,16,128]{2,1,0:T(8,128)} %get-tuple-element.13.fin), custom_call_target="tpu_custom_call" | custom-call | tf_op jit(solution)/shard_map/closing/pallas_call | solution.py:563

commit v5 on v4

--- a/solution.py
+++ b/solution.py
@@ -30,6 +30,13 @@
     sum_a, sum_b, recv_a2, recv_b2, zsend, zrecv, fin_t, fin_recv,
     lsem, osem, hs, hr, ps, pr, as_, ar, bs, br, a2s, a2r, b2s, b2r, zs, zr, fs, fr,
 ):
+    loads = [
+        pltpu.make_async_copy(source, target, lsem.at[n])
+        for n, (source, target) in enumerate(((feat_hbm, feat), (cot_hbm, cot), (w1_hbm, w1), (w2_hbm, w2)))
+    ]
+    for load in loads:
+        load.start()
+
     dp = lax.axis_index("dp")
     slab = lax.axis_index("slab")
     core = dp % 2
@@ -52,16 +59,9 @@
     f_peers = [dev(y_=(yc + d) % 8 // 2, core_=(yc + d) % 2) for d in range(1, 8)]
 
     barrier = pltpu.get_barrier_semaphore()
-    everyone = [(dp, after), (dp, before), peer] + x_peers + y_peers + z_peers + f_peers
+    everyone = [(dp, after), (dp, before)] + x_peers + z_peers + f_peers
     for d in everyone:
         pl.semaphore_signal(barrier, inc=1, device_id=d, device_id_type=MESH)
-
-    loads = [
-        pltpu.make_async_copy(source, target, lsem.at[n])
-        for n, (source, target) in enumerate(((feat_hbm, feat), (cot_hbm, cot), (w1_hbm, w1), (w2_hbm, w2)))
-    ]
-    for load in loads:
-        load.start()
 
     def remote(src, dst, send, recv, to):
         return pltpu.make_async_remote_copy(
@@ -403,9 +403,8 @@
     second = halo(pack2, hrecv2, 1)
     for copy in second:
         copy.start()
-    on(1, (pass_on, 0))
-
-    gradients(grad_one_at, 0, lambda n: on(1, (pass_on, 1)) if n == 2 else None)
+    gradients(grad_one_at, 0, lambda n: on(1, (pass_on, 0)) if n == 1 else None)
+    on(1, (pass_on, 1))
 
     finish_halo(second, hrecv2, t_ext)
     build(t_ext, 0)
@@ -419,9 +418,11 @@
     each(0, 3, lambda n: forward((3 * n, 3 * n + 1, 3 * n + 2), w2))
     on(0, (end_first, 0))
     on(1, (end_second, 0))
-    each(0, 3, lambda n: backward((3 * n, 3 * n + 1, 3 * n + 2), w1))
+    each(0, 1, lambda n: backward((3 * n, 3 * n + 1, 3 * n + 2), w1))
     on(0, (end_first, 1))
     on(1, (end_second, 1))
+    each(1, 3, lambda n: backward((3 * n, 3 * n + 1, 3 * n + 2), w1))
+    on(0, (end_second, 0))
     for k in range(4):
         rows = slice(k * ROWS, (k + 1) * ROWS)
         for n, acc in enumerate((acc_a, acc_b)):
@@ -436,7 +437,7 @@
     for store in stores:
         store.start()
 
-    on(0, (end_second, 0), (end_second, 1))
+    on(0, (end_second, 1))
     for _, copy in stage_z:
         copy.wait_recv()
     whole = total(zsend[z_hi, z_lo], *[zrecv[d] for d in range(7)]) * factor

time: 67.1 us -> 66.8 us (level); the launches traced: 65.8 us -> 66.4 us
  no operation moved by 1% of the time
where the time goes in v5:
time: 66.8 us; the launch traced here: 66.4 us
  Pallas kernels  65.1 us (97%)
  between operations  1.29 us (2%)
    pallas_call x1, Pallas kernels, per_device(): pl.pallas_call(lambda *refs: kernel(factor, *refs), out_shape=(big, big,...  63.2 us
    pallas_call x1, Pallas kernels, per_device(): pl.pallas_call(closing, out_shape=(big, big, piece, piece), in_specs=[vme...  1.94 us

profile of v5, /device:TPU:1, one launch (start us, length us, event | category | flops | bytes accessed | tf_op | source)
XLA Modules:
  0.0 66.4 jit_solution(12585274598590368026)
XLA Ops:
  1.3 63.2 %step.1 = (bf16[10,64,256]{2,1,0:T(8,128)(2,1)}, bf16[10,64,256]{2,1,0:T(8,128)(2,1)}, f32[8,16,128]{2,1,0:T(8,128)}) custom-call(s32[1,1]{1,0:T(1,128)S(6)} %copy.11.refs_0_, s32[2,2]{1,0:T(2,128)} %bitcast.15, s32[10,1,27]{2,1,0:T(1,128)} %bitcast.14, bf16[10,64,256]{2,1,0:T(8,128)(2,1)} %bitcast.12, bf16[10,64,256]{2,1,0:T(8,128)(2,1)} %bitcast.13, ...), custom_call_target="tpu_custom_call" | custom-call | tf_op jit(solution)/shard_map/step/pallas_call | solution.py:487
  64.5 1.9 %closing.1 = (bf16[10,64,256]{2,1,0:T(8,128)(2,1)}, bf16[10,64,256]{2,1,0:T(8,128)(2,1)}, f32[16,432]{1,0:T(8,128)}, f32[16,432]{1,0:T(8,128)}) custom-call(bf16[10,64,256]{2,1,0:T(8,128)(2,1)} %get-tuple-element.11.out_in, bf16[10,64,256]{2,1,0:T(8,128)(2,1)} %get-tuple-element.12.gf_in, f32[8,16,128]{2,1,0:T(8,128)} %get-tuple-element.13.fin), custom_call_target="tpu_custom_call" | custom-call | tf_op jit(solution)/shard_map/closing/pallas_call | solution.py:564

commit v6 on v5

--- a/solution.py
+++ b/solution.py
@@ -27,8 +27,9 @@
     out_hbm, gf_hbm, fin_ref,
     w1, w2, feat, cot, out_v, gf_v, nat, t_own, t_ext, pack, hrecv, t_own2, pack2, hrecv2, sel, win, acc_a, acc_b,
     hid_t, gh_t, mine, precv, relay_a, direct_a, summed_a, stage_a, relay_b, direct_b, summed_b, stage_b,
-    sum_a, sum_b, recv_a2, recv_b2, zsend, zrecv, fin_t, fin_recv,
-    lsem, osem, hs, hr, ps, pr, as_, ar, bs, br, a2s, a2r, b2s, b2r, zs, zr, fs, fr,
+    sum_a, sum_b, recv_a2, recv_b2, zsend, zrecv,
+    tail_z, tail_z_in, tail_x, tail_x_in, tail_y, tail_y_in, fin_t, fin_recv,
+    lsem, osem, hs, hr, ps, pr, as_, ar, bs, br, a2s, a2r, b2s, b2r, zs, zr, fs, fr, tzs, tzr, txs, txr, tys, tyr,
 ):
     loads = [
         pltpu.make_async_copy(source, target, lsem.at[n])
@@ -226,10 +227,10 @@
         return pl.ds(pl.multiple_of(start, 16), size)
 
     def slab_rows(zl, owner_x):
-        return rows_at(432 * (zl * 4 + owner_x), 432)
+        return rows_at(432 * (zl * 4 + owner_x), 384)
 
     def part_rows(zl, s, owner_y):
-        return rows_at(432 * (zl * 4 + s) + 112 * owner_y, 112)
+        return rows_at(432 * (zl * 4 + s) + 96 * owner_y, 96)
 
     LOW, HIGH = slice(0, 128), slice(128, 256)
     next_x, last_x, far_x = (x + 1) % 4, (x + 3) % 4, (x + 2) % 4
@@ -307,7 +308,7 @@
     for h in range(2):
         to_y = [
             remote(
-                sum_a.at[h, rows_at(112 * ((y + d) % 4), 112)], recv_a2.at[h, d - 1], a2s.at[h, d - 1], a2r.at[h, d - 1],
+                sum_a.at[h, rows_at(96 * ((y + d) % 4), 96)], recv_a2.at[h, d - 1], a2s.at[h, d - 1], a2r.at[h, d - 1],
                 y_peers[d - 1],
             )
             for d in (2, 1, 3)
@@ -328,8 +329,7 @@
             (HIGH, direct_a, summed_a, 0, 1),
         ):
             value = total(xy[slab_rows(h, x), lanes], a[h, a_buf], b[h, b_buf])
-            sum_a[h, 0:432, lanes] = value.astype(BF16)
-        sum_a[h, 432:448] = jnp.zeros((16, C), BF16)
+            sum_a[h, :, lanes] = value.astype(BF16)
         for copy in second_copies[h][0]:
             copy.start()
         for s in range(4):
@@ -348,7 +348,7 @@
     def end_second(h):
         for copy in second_copies[h][0]:
             copy.wait_recv()
-        full = total(sum_a[h, rows_at(112 * y, 112)], *[recv_a2[h, d] for d in range(3)]).astype(BF16)
+        full = total(sum_a[h, rows_at(96 * y, 96)], *[recv_a2[h, d] for d in range(3)]).astype(BF16)
         zsend[0, h], zsend[1, h] = full[:, LOW], full[:, HIGH]
         for copy in second_copies[h][1]:
             copy.wait_recv()
@@ -361,6 +361,48 @@
             def _():
                 copy.start()
 
+    tails_z = []
+    for d in (4, 3, 5, 2, 6, 1, 7):
+        to = (z + d) % 8
+        copy = remote(tail_z.at[to // 4, to % 4], tail_z_in.at[d - 1], tzs.at[d - 1], tzr.at[d - 1], z_peers[d - 1])
+        tails_z.append((to, copy))
+    tails_x = [
+        remote(tail_x.at[(x + d) % 4], tail_x_in.at[d - 1], txs.at[d - 1], txr.at[d - 1], x_peers[d - 1]) for d in (2, 1, 3)
+    ]
+    tails_y = [
+        remote(tail_y.at[(y + d) % 4], tail_y_in.at[d - 1], tys.at[d - 1], tyr.at[d - 1], y_peers[d - 1]) for d in (2, 1, 3)
+    ]
+
+    def pack_tail(s):
+        rows = xy[432 * s + 384 : 432 * s + 432]
+        tail_z[0, s // 4, s % 4], tail_z[1, s // 4, s % 4] = rows[:, LOW], rows[:, HIGH]
+
+    def start_tails(h):
+        for to, copy in tails_z:
+            outer = (to % 4 == 0) | (to % 4 == 3)
+
+            @pl.when(outer if h == 0 else jnp.logical_not(outer))
+            def _():
+                copy.start()
+
+    def tail_after_z(_):
+        for _, copy in tails_z:
+            copy.wait_recv()
+        for s in range(4):
+            tail_x[s] = total(tail_z[z_hi, z_lo, s], *[tail_z_in[d, s] for d in range(7)]).astype(BF16)
+        for copy in tails_x:
+            copy.start()
+
+    def tail_after_x(_):
+        for copy in tails_x:
+            copy.wait_recv()
+        value = total(tail_x[x], *[tail_x_in[d] for d in range(3)]).astype(BF16)
+        for part in range(3):
+            tail_y[part] = value[16 * part : 16 * part + 16]
+        tail_y[3] = jnp.zeros((16, 128), BF16)
+        for copy in tails_y:
+            copy.start()
+
     def on(which, *steps):
         @pl.when(core == which)
         def _():
@@ -375,6 +417,9 @@
                 join(g)
             for s in READY[n]:
                 start_slab(s)
+                pack_tail(s)
+            if n in (2, 4):
+                start_tails(0 if n == 2 else 1)
 
         def send(g):
             to_peer(g).start()
@@ -389,7 +434,6 @@
             between(n)
         on(keeper, (finish, 4))
 
-    xy[6912:6928] = jnp.zeros((16, C), BF16)
     gradients(grad_two_at, 1, lambda n: None)
 
     sides(lambda gs: backward(gs, w2))
@@ -403,26 +447,21 @@
     second = halo(pack2, hrecv2, 1)
     for copy in second:
         copy.start()
-    gradients(grad_one_at, 0, lambda n: on(1, (pass_on, 0)) if n == 1 else None)
-    on(1, (pass_on, 1))
+    on(1, (pass_on, 0))
+
+    gradients(grad_one_at, 0, lambda n: on(1, (pass_on, 1)) if n == 2 else None)
 
     finish_halo(second, hrecv2, t_ext)
-    build(t_ext, 0)
+    each(0, 3, lambda dx: build(t_ext, dx))
     on(0, (pass_on, 0))
     on(1, (end_first, 0))
-    each(1, 3, lambda dx: build(t_ext, dx))
-    on(0, (pass_on, 1))
-    on(1, (end_first, 1))
     acc_a[...] = jnp.zeros_like(acc_a)
     acc_b[...] = jnp.zeros_like(acc_b)
     each(0, 3, lambda n: forward((3 * n, 3 * n + 1, 3 * n + 2), w2))
-    on(0, (end_first, 0))
-    on(1, (end_second, 0))
-    each(0, 1, lambda n: backward((3 * n, 3 * n + 1, 3 * n + 2), w1))
-    on(0, (end_first, 1))
-    on(1, (end_second, 1))
-    each(1, 3, lambda n: backward((3 * n, 3 * n + 1, 3 * n + 2), w1))
-    on(0, (end_second, 0))
+    on(0, (pass_on, 1))
+    on(1, (end_first, 1), (end_second, 0), (tail_after_z, 0))
+    each(0, 3, lambda n: backward((3 * n, 3 * n + 1, 3 * n + 2), w1))
+    on(1, (end_second, 1), (tail_after_x, 0))
     for k in range(4):
         rows = slice(k * ROWS, (k + 1) * ROWS)
         for n, acc in enumerate((acc_a, acc_b)):
@@ -437,11 +476,14 @@
     for store in stores:
         store.start()
 
-    on(0, (end_second, 1))
+    on(0, (end_first, 0), (tail_after_z, 0), (end_first, 1), (end_second, 0), (tail_after_x, 0), (end_second, 1))
+    for copy in tails_y:
+        copy.wait_recv()
+    tail = total(tail_y[y], *[tail_y_in[d] for d in range(3)]) * factor
     for _, copy in stage_z:
         copy.wait_recv()
     whole = total(zsend[z_hi, z_lo], *[zrecv[d] for d in range(7)]) * factor
-    padded = jnp.concatenate([whole, jnp.zeros((16, 128), F32)], axis=0)
+    padded = jnp.concatenate([whole, tail, jnp.zeros((16, 128), F32)], axis=0)
     fin_t[...] = padded.T.reshape(8, 16, 128)
 
     stage_f = []
@@ -456,7 +498,7 @@
     for d in range(1, 8):
         fin_ref[(yc + 8 - d) % 8] = fin_recv[d - 1]
 
-    sent = list(first) + list(second) + [copy for _, copy in stage_z] + stage_f
+    sent = list(first) + list(second) + [copy for _, copy in stage_z + tails_z] + stage_f + tails_x + tails_y
     for h in range(2):
         sent += [copy for group in copies_of[h].values() for copy in group]
         sent += second_copies[h][0] + second_copies[h][1]
@@ -473,8 +515,10 @@
     gf_ref[...] = gf_in[...]
     for src_core, target in ((0, g1_ref), (1, g2_ref)):
         for src_y in range(4):
-            size = 112 if src_y < 3 else 96
-            target[:, 112 * src_y : 112 * src_y + size] = fin[src_y * 2 + src_core, :, 0:size]
+            part = fin[src_y * 2 + src_core]
+            target[:, 96 * src_y : 96 * src_y + 96] = part[:, 0:96]
+            if src_y < 3:
+                target[:, 384 + 16 * src_y : 400 + 16 * src_y] = part[:, 96:112]
 
 
 def per_device(features, cotangent, neighbour_table, send_lists, block_counts, weight_one, weight_two):
@@ -510,22 +554,28 @@
             pltpu.VMEM((640, C), F32),
             pltpu.VMEM((C, 640), BF16),
             pltpu.VMEM((C, 640), BF16),
-            pltpu.VMEM((2, 6928, C), BF16),
+            pltpu.VMEM((2, 6912, C), BF16),
             pltpu.VMEM((6912, C), BF16),
-            pltpu.VMEM((2, 2, 432, 128), BF16),
-            pltpu.VMEM((2, 2, 432, 128), BF16),
-            pltpu.VMEM((2, 2, 432, 128), BF16),
-            pltpu.VMEM((2, 2, 432, 128), BF16),
-            pltpu.VMEM((2, 2, 4, 112, 128), BF16),
-            pltpu.VMEM((2, 2, 4, 112, 128), BF16),
-            pltpu.VMEM((2, 2, 4, 112, 128), BF16),
-            pltpu.VMEM((2, 2, 4, 112, 128), BF16),
-            pltpu.VMEM((2, 448, C), BF16),
-            pltpu.VMEM((2, 4, 112, C), BF16),
-            pltpu.VMEM((2, 3, 112, C), BF16),
-            pltpu.VMEM((2, 3, 112, C), BF16),
-            pltpu.VMEM((2, 4, 112, 128), BF16),
-            pltpu.VMEM((7, 112, 128), BF16),
+            pltpu.VMEM((2, 2, 384, 128), BF16),
+            pltpu.VMEM((2, 2, 384, 128), BF16),
+            pltpu.VMEM((2, 2, 384, 128), BF16),
+            pltpu.VMEM((2, 2, 384, 128), BF16),
+            pltpu.VMEM((2, 2, 4, 96, 128), BF16),
+            pltpu.VMEM((2, 2, 4, 96, 128), BF16),
+            pltpu.VMEM((2, 2, 4, 96, 128), BF16),
+            pltpu.VMEM((2, 2, 4, 96, 128), BF16),
+            pltpu.VMEM((2, 384, C), BF16),
+            pltpu.VMEM((2, 4, 96, C), BF16),
+            pltpu.VMEM((2, 3, 96, C), BF16),
+            pltpu.VMEM((2, 3, 96, C), BF16),
+            pltpu.VMEM((2, 4, 96, 128), BF16),
+            pltpu.VMEM((7, 96, 128), BF16),
+            pltpu.VMEM((2, 4, 4, 48, 128), BF16),
+            pltpu.VMEM((7, 4, 48, 128), BF16),
+            pltpu.VMEM((4, 48, 128), BF16),
+            pltpu.VMEM((3, 48, 128), BF16),
+            pltpu.VMEM((4, 16, 128), BF16),
+            pltpu.VMEM((3, 16, 128), BF16),
             pltpu.VMEM((8, 16, 128), F32),
             pltpu.VMEM((7, 16, 128), F32),
             dma((4,)),
@@ -546,6 +596,12 @@
             dma((7,)),
             dma((7,)),
             dma((7,)),
+            dma((7,)),
+            dma((7,)),
+            dma((3,)),
+            dma((3,)),
+            dma((3,)),
+            dma((3,)),
         ],
         compiler_params=pltpu.CompilerParams(
             collective_id=0, has_side_effects=True, vmem_limit_bytes=60 * 1024 * 1024

time: 66.8 us -> 65.7 us (0.984)
  Pallas kernels: 65.1 us -> 64.3 us
    pallas_call x1, Pallas kernels: 63.2 us -> 62.4 us  [per_device(): pl.pallas_call(lambda *refs: kernel(factor, *refs), out_shape=(big, big,...]
where the time goes in v6:
time: 65.7 us; the launch traced here: 65.6 us
  Pallas kernels  64.3 us (98%)
  between operations  1.29 us (2%)
    pallas_call x1, Pallas kernels, per_device(): pl.pallas_call(lambda *refs: kernel(factor, *refs), out_shape=(big, big,...  62.4 us
    pallas_call x1, Pallas kernels, per_device(): pl.pallas_call(closing, out_shape=(big, big, piece, piece), in_specs=[vme...  1.94 us

profile of v6, /device:TPU:1, one launch (start us, length us, event | category | flops | bytes accessed | tf_op | source)
XLA Modules:
  0.0 65.6 jit_solution(537441864968744338)
XLA Ops:
  1.3 62.4 %step.1 = (bf16[10,64,256]{2,1,0:T(8,128)(2,1)}, bf16[10,64,256]{2,1,0:T(8,128)(2,1)}, f32[8,16,128]{2,1,0:T(8,128)}) custom-call(s32[1,1]{1,0:T(1,128)S(6)} %copy.11.refs_0_, s32[2,2]{1,0:T(2,128)} %bitcast.15, s32[10,1,27]{2,1,0:T(1,128)} %bitcast.14, bf16[10,64,256]{2,1,0:T(8,128)(2,1)} %bitcast.12, bf16[10,64,256]{2,1,0:T(8,128)(2,1)} %bitcast.13, ...), custom_call_target="tpu_custom_call" | custom-call | tf_op jit(solution)/shard_map/step/pallas_call | solution.py:531
  63.6 1.9 %closing.1 = (bf16[10,64,256]{2,1,0:T(8,128)(2,1)}, bf16[10,64,256]{2,1,0:T(8,128)(2,1)}, f32[16,432]{1,0:T(8,128)}, f32[16,432]{1,0:T(8,128)}) custom-call(bf16[10,64,256]{2,1,0:T(8,128)(2,1)} %get-tuple-element.11.out_in, bf16[10,64,256]{2,1,0:T(8,128)(2,1)} %get-tuple-element.12.gf_in, f32[8,16,128]{2,1,0:T(8,128)} %get-tuple-element.13.fin), custom_call_target="tpu_custom_call" | custom-call | tf_op jit(solution)/shard_map/closing/pallas_call | solution.py:620

commit v7 on v6

--- a/solution.py
+++ b/solution.py
@@ -453,15 +453,16 @@
 
     finish_halo(second, hrecv2, t_ext)
     each(0, 3, lambda dx: build(t_ext, dx))
-    on(0, (pass_on, 0))
+    on(0, (pass_on, 0), (pass_on, 1))
     on(1, (end_first, 0))
     acc_a[...] = jnp.zeros_like(acc_a)
     acc_b[...] = jnp.zeros_like(acc_b)
     each(0, 3, lambda n: forward((3 * n, 3 * n + 1, 3 * n + 2), w2))
-    on(0, (pass_on, 1))
+    on(0, (end_first, 0), (tail_after_z, 0), (end_first, 1))
     on(1, (end_first, 1), (end_second, 0), (tail_after_z, 0))
     each(0, 3, lambda n: backward((3 * n, 3 * n + 1, 3 * n + 2), w1))
     on(1, (end_second, 1), (tail_after_x, 0))
+    on(0, (end_second, 0), (tail_after_x, 0), (end_second, 1))
     for k in range(4):
         rows = slice(k * ROWS, (k + 1) * ROWS)
         for n, acc in enumerate((acc_a, acc_b)):
@@ -476,7 +477,6 @@
     for store in stores:
         store.start()
 
-    on(0, (end_first, 0), (tail_after_z, 0), (end_first, 1), (end_second, 0), (tail_after_x, 0), (end_second, 1))
     for copy in tails_y:
         copy.wait_recv()
     tail = total(tail_y[y], *[tail_y_in[d] for d in range(3)]) * factor

time: 65.7 us -> 64.5 us (0.982)
  Pallas kernels: 64.3 us -> 63 us
    pallas_call x1, Pallas kernels: 62.4 us -> 61.1 us  [per_device(): pl.pallas_call(lambda *refs: kernel(factor, *refs), out_shape=(big, big,...]
where the time goes in v7:
time: 64.5 us; the launch traced here: 64.3 us
  Pallas kernels  63 us (98%)
  between operations  1.29 us (2%)
    pallas_call x1, Pallas kernels, per_device(): pl.pallas_call(lambda *refs: kernel(factor, *refs), out_shape=(big, big,...  61.1 us
    pallas_call x1, Pallas kernels, per_device(): pl.pallas_call(closing, out_shape=(big, big, piece, piece), in_specs=[vme...  1.94 us

profile of v7, /device:TPU:1, one launch (start us, length us, event | category | flops | bytes accessed | tf_op | source)
XLA Modules:
  0.0 64.3 jit_solution(17469000857090041489)
XLA Ops:
  1.3 61.1 %step.1 = (bf16[10,64,256]{2,1,0:T(8,128)(2,1)}, bf16[10,64,256]{2,1,0:T(8,128)(2,1)}, f32[8,16,128]{2,1,0:T(8,128)}) custom-call(s32[1,1]{1,0:T(1,128)S(6)} %copy.11.refs_0_, s32[2,2]{1,0:T(2,128)} %bitcast.15, s32[10,1,27]{2,1,0:T(1,128)} %bitcast.14, bf16[10,64,256]{2,1,0:T(8,128)(2,1)} %bitcast.12, bf16[10,64,256]{2,1,0:T(8,128)(2,1)} %bitcast.13, ...), custom_call_target="tpu_custom_call" | custom-call | tf_op jit(solution)/shard_map/step/pallas_call | solution.py:531
  62.4 1.9 %closing.1 = (bf16[10,64,256]{2,1,0:T(8,128)(2,1)}, bf16[10,64,256]{2,1,0:T(8,128)(2,1)}, f32[16,432]{1,0:T(8,128)}, f32[16,432]{1,0:T(8,128)}) custom-call(bf16[10,64,256]{2,1,0:T(8,128)(2,1)} %get-tuple-element.11.out_in, bf16[10,64,256]{2,1,0:T(8,128)(2,1)} %get-tuple-element.12.gf_in, f32[8,16,128]{2,1,0:T(8,128)} %get-tuple-element.13.fin), custom_call_target="tpu_custom_call" | custom-call | tf_op jit(solution)/shard_map/closing/pallas_call | solution.py:620

commit v8 on v7

--- a/solution.py
+++ b/solution.py
@@ -447,9 +447,8 @@
     second = halo(pack2, hrecv2, 1)
     for copy in second:
         copy.start()
-    on(1, (pass_on, 0))
-
-    gradients(grad_one_at, 0, lambda n: on(1, (pass_on, 1)) if n == 2 else None)
+    gradients(grad_one_at, 0, lambda n: on(1, (pass_on, 0)) if n == 1 else None)
+    on(1, (pass_on, 1))
 
     finish_halo(second, hrecv2, t_ext)
     each(0, 3, lambda dx: build(t_ext, dx))
@@ -493,12 +492,7 @@
     for copy in stage_f:
         copy.start()
     fin_ref[yc] = fin_t[yc]
-    for d in range(1, 8):
-        stage_f[d - 1].wait_recv()
-    for d in range(1, 8):
-        fin_ref[(yc + 8 - d) % 8] = fin_recv[d - 1]
-
-    sent = list(first) + list(second) + [copy for _, copy in stage_z + tails_z] + stage_f + tails_x + tails_y
+    sent = list(first) + list(second) + [copy for _, copy in stage_z + tails_z] + tails_x + tails_y
     for h in range(2):
         sent += [copy for group in copies_of[h].values() for copy in group]
         sent += second_copies[h][0] + second_copies[h][1]
@@ -508,6 +502,12 @@
         store.wait()
 
     each(0, 9, lambda g: to_peer(g).wait_send())
+    for d in range(1, 8):
+        stage_f[d - 1].wait_recv()
+    for d in range(1, 8):
+        fin_ref[(yc + 8 - d) % 8] = fin_recv[d - 1]
+    for copy in stage_f:
+        copy.wait_send()
 
 
 def closing(out_in, gf_in, fin, out_ref, gf_ref, g1_ref, g2_ref):

time: 64.5 us -> 65.2 us (1.011)
  Pallas kernels: 63 us -> 63.8 us
    pallas_call x1, Pallas kernels: 61.1 us -> 61.9 us  [per_device(): pl.pallas_call(lambda *refs: kernel(factor, *refs), out_shape=(big, big,...]
where the time goes in v8:
time: 65.2 us; the launch traced here: 65.1 us
  Pallas kernels  63.8 us (98%)
  between operations  1.29 us (2%)
    pallas_call x1, Pallas kernels, per_device(): pl.pallas_call(lambda *refs: kernel(factor, *refs), out_shape=(big, big,...  61.9 us
    pallas_call x1, Pallas kernels, per_device(): pl.pallas_call(closing, out_shape=(big, big, piece, piece), in_specs=[vme...  1.94 us

profile of v8, /device:TPU:1, one launch (start us, length us, event | category | flops | bytes accessed | tf_op | source)
XLA Modules:
  0.0 65.1 jit_solution(15405559022348184063)
XLA Ops:
  1.3 61.9 %step.1 = (bf16[10,64,256]{2,1,0:T(8,128)(2,1)}, bf16[10,64,256]{2,1,0:T(8,128)(2,1)}, f32[8,16,128]{2,1,0:T(8,128)}) custom-call(s32[1,1]{1,0:T(1,128)S(6)} %copy.11.refs_0_, s32[2,2]{1,0:T(2,128)} %bitcast.15, s32[10,1,27]{2,1,0:T(1,128)} %bitcast.14, bf16[10,64,256]{2,1,0:T(8,128)(2,1)} %bitcast.12, bf16[10,64,256]{2,1,0:T(8,128)(2,1)} %bitcast.13, ...), custom_call_target="tpu_custom_call" | custom-call | tf_op jit(solution)/shard_map/step/pallas_call | solution.py:531
  63.1 1.9 %closing.1 = (bf16[10,64,256]{2,1,0:T(8,128)(2,1)}, bf16[10,64,256]{2,1,0:T(8,128)(2,1)}, f32[16,432]{1,0:T(8,128)}, f32[16,432]{1,0:T(8,128)}) custom-call(bf16[10,64,256]{2,1,0:T(8,128)(2,1)} %get-tuple-element.11.out_in, bf16[10,64,256]{2,1,0:T(8,128)(2,1)} %get-tuple-element.12.gf_in, f32[8,16,128]{2,1,0:T(8,128)} %get-tuple-element.13.fin), custom_call_target="tpu_custom_call" | custom-call | tf_op jit(solution)/shard_map/closing/pallas_call | solution.py:620

commit v9 on v8

--- a/solution.py
+++ b/solution.py
@@ -447,8 +447,9 @@
     second = halo(pack2, hrecv2, 1)
     for copy in second:
         copy.start()
-    gradients(grad_one_at, 0, lambda n: on(1, (pass_on, 0)) if n == 1 else None)
-    on(1, (pass_on, 1))
+    on(1, (pass_on, 0))
+
+    gradients(grad_one_at, 0, lambda n: on(1, (pass_on, 1)) if n == 2 else None)
 
     finish_halo(second, hrecv2, t_ext)
     each(0, 3, lambda dx: build(t_ext, dx))

time: 65.2 us -> 64.3 us (0.986)
  Pallas kernels: 63.8 us -> 62.8 us
    pallas_call x1, Pallas kernels: 61.9 us -> 60.9 us  [per_device(): pl.pallas_call(lambda *refs: kernel(factor, *refs), out_shape=(big, big,...]
where the time goes in v9:
time: 64.3 us; the launch traced here: 64.1 us
  Pallas kernels  62.8 us (98%)
  between operations  1.29 us (2%)
    pallas_call x1, Pallas kernels, per_device(): pl.pallas_call(lambda *refs: kernel(factor, *refs), out_shape=(big, big,...  60.9 us
    pallas_call x1, Pallas kernels, per_device(): pl.pallas_call(closing, out_shape=(big, big, piece, piece), in_specs=[vme...  1.94 us

profile of v9, /device:TPU:1, one launch (start us, length us, event | category | flops | bytes accessed | tf_op | source)
XLA Modules:
  0.0 64.1 jit_solution(14443106411001319734)
XLA Ops:
  1.3 60.9 %step.1 = (bf16[10,64,256]{2,1,0:T(8,128)(2,1)}, bf16[10,64,256]{2,1,0:T(8,128)(2,1)}, f32[8,16,128]{2,1,0:T(8,128)}) custom-call(s32[1,1]{1,0:T(1,128)S(6)} %copy.11.refs_0_, s32[2,2]{1,0:T(2,128)} %bitcast.15, s32[10,1,27]{2,1,0:T(1,128)} %bitcast.14, bf16[10,64,256]{2,1,0:T(8,128)(2,1)} %bitcast.12, bf16[10,64,256]{2,1,0:T(8,128)(2,1)} %bitcast.13, ...), custom_call_target="tpu_custom_call" | custom-call | tf_op jit(solution)/shard_map/step/pallas_call | solution.py:532
  62.2 1.9 %closing.1 = (bf16[10,64,256]{2,1,0:T(8,128)(2,1)}, bf16[10,64,256]{2,1,0:T(8,128)(2,1)}, f32[16,432]{1,0:T(8,128)}, f32[16,432]{1,0:T(8,128)}) custom-call(bf16[10,64,256]{2,1,0:T(8,128)(2,1)} %get-tuple-element.11.out_in, bf16[10,64,256]{2,1,0:T(8,128)(2,1)} %get-tuple-element.12.gf_in, f32[8,16,128]{2,1,0:T(8,128)} %get-tuple-element.13.fin), custom_call_target="tpu_custom_call" | custom-call | tf_op jit(solution)/shard_map/closing/pallas_call | solution.py:621
